TPU v7x, 512 devices: a whole 4x4x16 slice. The times are simulated.
512 devices in a mesh: feeder: 8 (over z_hi, y), tm: 64 (over z_lo, x, core).
Axes of the slice: x: 4, y: 4, z: 16 (z_hi: 2, z_lo: 8; z = z_hi * 8 + z_lo), core: 2. Of those that a mesh axis runs over, the one named last changes fastest.
Arguments:
- observed: bfloat16 [24576, 32768], P('feeder', 'tm'), may hold values from -16 to 16
- mask_words: int32 [24576, 4096], P('feeder', 'tm'), may hold values from 0 to 255, as said below
- feeder_factor: float32 [24576, 64], P('feeder'), may hold values from -6 to 6
- time_factor: float32 [64, 32768], P(None, 'tm'), may hold values from -0.75 to 0.75
- ar_weight: float32 [10, 64], replicated, may hold values from -0.5 to 0.5
- lags: int32 [10], replicated, may hold values from 1 to 1440, as said below
- moment_first: float32 [24576, 64], P(('feeder', 'tm')), may hold values from -0.6 to 0.6
- moment_second: float32 [24576, 64], P(('feeder', 'tm')), may hold values from 0.01 to 1
Outputs:
- new_factor: float32 [24576, 64], P(('feeder', 'tm'))
- new_first: float32 [24576, 64], P(('feeder', 'tm'))
- new_second: float32 [24576, 64], P(('feeder', 'tm'))
- time_grad: float32 [64, 32768], P('feeder', 'tm')
Inputs may be any that keep to these rules, and one draw needn't show every extreme that they name: `mask_words`: bit b of word w of a feeder's row tells whether minute 8 w + b is observed (1) or not (0). Eight lags of 1 to 12, one lag between 30 and 90, and one lag of exactly 1440; lags may repeat.
All inputs are finite; a program needn't handle non-finite values.
Results may differ from a plain program's by a relative error of at most 0.00065.
Values sent between devices are 32-bit elements; how exact they have to be, the bound alone decides.
No kernel may reach another device: no remote copies, remote signals or barrier semaphores. Data moves between devices by JAX's collectives and lax.ppermute only.
A program may use at most 64 MiB of HBM per device.

v0:
```python
import jax
import jax.numpy as jnp
from jax import lax
from jax.sharding import PartitionSpec as P

LAGMAX = 1440


DATA_WEIGHT = 1.0 / 64.0
LAM_F = 0.1
LAM_X = 0.01
LAM_AR = 8.0
BETA_ONE = 0.9
BETA_TWO = 0.999
BIAS_FIRST = 1.0 - 0.9**8
BIAS_SECOND = 1.0 - 0.999**8
LEARNING_RATE = 0.05
ADAM_EPS = 1e-08


def from_behind(value, axis, steps):
    count = lax.axis_size(axis)
    first, last = (max(0, -steps), min(count, count - steps))
    return lax.ppermute(value, axis, [(source, source + steps) for source in range(first, last)])


def unpack_mask(words):
    shifts = jnp.arange(8, dtype=jnp.int32)
    bits = words[:, :, None] >> shifts & 1
    return bits.reshape(words.shape[0], words.shape[1] * 8).astype(jnp.float32)


def lagged(source, offset, width):
    return lax.dynamic_slice_in_dim(source, offset, width, 1)


def ar_adjoint(rank_rows, weights, lags, column_start):
    ranks, width = rank_rows.shape
    hop_count = -(-LAGMAX // width)
    earlier = []
    for distance in range(hop_count, 0, -1):
        earlier.append(from_behind(rank_rows, "tm", distance))
    extended = jnp.concatenate(earlier + [rank_rows], axis=1)
    anchor = hop_count * width
    predicted = jnp.zeros_like(rank_rows)
    for lag_index in range(lags.shape[0]):
        predicted = predicted + weights[lag_index][:, None] * lagged(
            extended, anchor - lags[lag_index], width
        )
    columns = column_start + jnp.arange(width, dtype=jnp.int32)
    errors = jnp.where(columns[None, :] >= LAGMAX, rank_rows - predicted, 0.0)
    later = []
    for distance in range(1, hop_count + 1):
        later.append(from_behind(errors, "tm", -distance))
    ahead = jnp.concatenate([errors] + later, axis=1)
    carried = jnp.zeros_like(rank_rows)
    for lag_index in range(lags.shape[0]):
        carried = carried + weights[lag_index][:, None] * lagged(ahead, lags[lag_index], width)
    return errors - carried


def per_device(
    observed, mask_words, feeder_factor, time_factor, ar_weight, lags, moment_first, moment_second
):
    feeder_rows, span_dev = observed.shape
    ranks = time_factor.shape[0]
    observed_mask = unpack_mask(mask_words)
    factor_half = feeder_factor.astype(jnp.bfloat16)
    time_half = time_factor.astype(jnp.bfloat16)
    predicted = jnp.dot(factor_half, time_half, preferred_element_type=jnp.float32)
    residual = (observed_mask * (predicted - observed.astype(jnp.float32))).astype(jnp.bfloat16)
    factor_part = DATA_WEIGHT * lax.dot_general(
        residual, time_half, (((1,), (1,)), ((), ())), preferred_element_type=jnp.float32
    )
    time_part = DATA_WEIGHT * lax.dot_general(
        factor_half, residual, (((0,), (0,)), ((), ())), preferred_element_type=jnp.float32
    )
    tm_count = lax.axis_size("tm")
    tm_place = lax.axis_index("tm")
    share_rows = feeder_rows // tm_count
    summed = lax.psum(factor_part, "tm")
    grad_share = lax.dynamic_slice_in_dim(summed, tm_place * share_rows, share_rows, 0)
    own_factor = lax.dynamic_slice_in_dim(feeder_factor, tm_place * share_rows, share_rows, 0)
    factor_grad = grad_share + LAM_F * own_factor
    new_first = BETA_ONE * moment_first + (1.0 - BETA_ONE) * factor_grad
    new_second = BETA_TWO * moment_second + (1.0 - BETA_TWO) * factor_grad * factor_grad
    update = (
        LEARNING_RATE * (new_first / BIAS_FIRST) / (jnp.sqrt(new_second / BIAS_SECOND) + ADAM_EPS)
    )
    new_factor = own_factor - update
    feeder_count = lax.axis_size("feeder")
    feeder_place = lax.axis_index("feeder")
    band = ranks // feeder_count
    column_start = tm_place * span_dev
    time_total = lax.psum(time_part, "feeder")
    adjoint = ar_adjoint(time_factor, ar_weight, lags, column_start)
    full_grad = time_total + LAM_AR * adjoint + LAM_X * time_factor
    time_grad = lax.dynamic_slice_in_dim(full_grad, feeder_place * band, band, 0)
    return (new_factor, new_first, new_second, time_grad)


def solution(mesh):
    placed = (
        P("feeder", "tm"),
        P("feeder", "tm"),
        P("feeder", None),
        P(None, "tm"),
        P(),
        P(),
        P(("feeder", "tm"), None),
        P(("feeder", "tm"), None),
    )
    return jax.shard_map(
        per_device,
        mesh=mesh,
        in_specs=placed,
        out_specs=(
            P(("feeder", "tm"), None),
            P(("feeder", "tm"), None),
            P(("feeder", "tm"), None),
            P("feeder", "tm"),
        ),
        check_vma=False,
    )
```

profile of v0, /device:TPU:1, one launch (start us, length us, event | category | flops | bytes accessed | tf_op | source)
XLA Modules:
  0.0 1029.0 jit_solution(8480299729980956916)
XLA Ops:
  7.2 0.0 copy-start
  7.2 0.0 all-reduce.5.cloned.1.call-start
  7.2 6.2 collective-permute-start
  13.4 2.2 collective-permute-start.1
  15.6 2.2 collective-permute-start.2
  17.8 0.0 copy-done
  17.8 3.5 broadcast_bitcast_fusion
  21.3 0.0 copy-start.2
  21.3 0.0 copy-start.3
  21.3 6.6 copy.15
  28.0 0.1 shift_right_arithmetic.23
  28.1 0.0 copy-done.2
  28.1 0.0 copy-done.3
  28.1 5.5 multiply_convert_fusion
  33.6 0.0 copy-start.1
  33.7 1.6 copy-done.1
  35.3 0.0 copy-start.7
  35.3 0.0 copy-start.4
  35.3 1.3 fusion
  36.6 0.0 all-reduce.5.cloned.1.call-update
  36.6 0.0 all-reduce.3.cloned.1.call-start
  36.7 0.0 copy-done.7
  36.7 0.0 copy-done.4
  36.7 0.7 fusion.10
  49.9 0.0 collective-permute-done
  49.9 0.0 collective-permute-done.1
  49.9 0.0 collective-permute-done.2
  50.0 0.6 subtract_select_fusion
  50.6 1.3 collective-permute-start.5
  51.9 1.3 collective-permute-start.4
  53.2 2.2 collective-permute-start.3
  55.4 4.0 convolution_multiply_fusion
  59.4 0.0 copy-start.5
  59.4 0.0 copy-start.6
  59.4 0.0 all-reduce.3.cloned.1.call-update
  71.9 0.1 constant_dynamic-slice_fusion
  71.9 0.1 copy.16
  72.0 0.1 dynamic-slice
  78.3 0.0 collective-permute-done.5
  78.3 0.0 collective-permute-done.4
  78.3 0.0 collective-permute-done.3
  78.4 0.5 multiply_add_fusion
  78.9 107.4 %all-reduce.5.cloned.1.call-done = f32[64,512]{1,0:T(8,128)} async-done(((f32[64,512]{1,0:T(8,128)}), f32[64,512]{1,0:T(8,128)}) %all-reduce.5.cloned.1.call-update) | async-done | bytes 131088 | tf_op jit(solution)/shard_map/psum | solution.py:95
  186.3 1.4 fusion.6
  187.7 833.1 %all-reduce.3.cloned.1.call-done = f32[3072,64]{1,0:T(8,128)} async-done(((f32[3072,64]{1,0:T(8,128)}), f32[3072,64]{1,0:T(8,128)}) %all-reduce.3.cloned.1.call-update) | async-done | bytes 786448 | tf_op jit(solution)/shard_map/psum | solution.py:81
  1020.8 0.0 copy-done.5
  1020.8 0.0 copy-done.6
  1020.8 1.4 divide_subtract_fusion
  (8 shorter events, 0.1 us)
Async XLA Ops:
  7.2 10.7 %copy-start = (s32[3072,64]{0,1:T(8,128)S(1)}, s32[3072,64]{0,1:T(8,128)}, u32[]{:S(2)}) copy-start(s32[3072,64]{0,1:T(8,128)} %param.9) | copy-start | bytes 2359300
  7.2 179.1 %all-reduce.5.cloned.1.call-start = ((), (), s32[]{:S(2)}) async-start(), calls=%async_computation.1 | async-start | bytes 262144 | tf_op jit(solution)/shard_map/psum | solution.py:95
  7.2 42.7 %collective-permute-start = (f32[64,512]{1,0:T(8,128)}, f32[64,512]{1,0:T(8,128)S(1)}, u32[]{:S(2)}, u32[]{:S(2)}) collective-permute-start(f32[64,512]{1,0:T(8,128)} %param.11), channel_id=1, source_target_pairs={{0,3},{1,4},{2,5},{3,6},{4,7},{5,8},{6,9},{7,10},{8,11},{9,12},{10... | collective-permute-start | bytes 393224 | tf_op jit(solution)/shard_map/ppermute | solution.py:24
  13.4 36.5 %collective-permute-start.1 = (f32[64,512]{1,0:T(8,128)}, f32[64,512]{1,0:T(8,128)S(1)}, u32[]{:S(2)}, u32[]{:S(2)}) collective-permute-start(f32[64,512]{1,0:T(8,128)} %param.11), channel_id=1, source_target_pairs={{0,2},{1,3},{2,4},{3,5},{4,6},{5,7},{6,8},{7,9},{8,10},{9,11},{10,... | collective-permute-start | bytes 393224 | tf_op jit(solution)/shard_map/ppermute | solution.py:24
  15.6 34.3 %collective-permute-start.2 = (f32[64,512]{1,0:T(8,128)}, f32[64,512]{1,0:T(8,128)S(1)}, u32[]{:S(2)}, u32[]{:S(2)}) collective-permute-start(f32[64,512]{1,0:T(8,128)} %param.11), channel_id=1, source_target_pairs={{0,1},{1,2},{2,3},{3,4},{4,5},{5,6},{6,7},{7,8},{8,9},{9,10},{10,1... | collective-permute-start | bytes 393224 | tf_op jit(solution)/shard_map/ppermute | solution.py:24
  21.3 6.7 copy-start.2
  21.3 6.7 copy-start.3
  33.6 1.6 copy-start.1
  35.3 1.4 copy-start.7
  35.3 1.4 copy-start.4
  36.6 984.2 %all-reduce.3.cloned.1.call-start = ((), (), s32[]{:S(2)}) async-start(), calls=%async_computation | async-start | bytes 3145728 | tf_op jit(solution)/shard_map/psum | solution.py:81
  50.6 27.8 %collective-permute-start.5 = (f32[64,512]{1,0:T(8,128)S(1)}, f32[64,512]{1,0:T(8,128)S(1)}, u32[]{:S(2)}, u32[]{:S(2)}) collective-permute-start(f32[64,512]{1,0:T(8,128)S(1)} %subtract_select_fusion), channel_id=1, source_target_pairs={{3,0},{4,1},{5,2},{6,3},{7,4},{8,5},{9,6},{10,7},{11,8},{12,9},{13... | collective-permute-start | bytes 393224 | tf_op jit(solution)/shard_map/ppermute | solution.py:24
  51.9 26.5 %collective-permute-start.4 = (f32[64,512]{1,0:T(8,128)S(1)}, f32[64,512]{1,0:T(8,128)S(1)}, u32[]{:S(2)}, u32[]{:S(2)}) collective-permute-start(f32[64,512]{1,0:T(8,128)S(1)} %subtract_select_fusion), channel_id=1, source_target_pairs={{2,0},{3,1},{4,2},{5,3},{6,4},{7,5},{8,6},{9,7},{10,8},{11,9},{12,... | collective-permute-start | bytes 393224 | tf_op jit(solution)/shard_map/ppermute | solution.py:24
  53.2 25.2 %collective-permute-start.3 = (f32[64,512]{1,0:T(8,128)S(1)}, f32[64,512]{1,0:T(8,128)S(1)}, u32[]{:S(2)}, u32[]{:S(2)}) collective-permute-start(f32[64,512]{1,0:T(8,128)S(1)} %subtract_select_fusion), channel_id=1, source_target_pairs={{1,0},{2,1},{3,2},{4,3},{5,4},{6,5},{7,6},{8,7},{9,8},{10,9},{11,1... | collective-permute-start | bytes 393224 | tf_op jit(solution)/shard_map/ppermute | solution.py:24
  59.4 961.4 %copy-start.5 = (f32[48,64]{1,0:T(8,128)S(1)}, f32[48,64]{1,0:T(8,128)}, u32[]{:S(2)}) copy-start(f32[48,64]{1,0:T(8,128)} %param.14) | copy-start | bytes 36868
  59.4 961.4 %copy-start.6 = (f32[48,64]{1,0:T(8,128)S(1)}, f32[48,64]{1,0:T(8,128)}, u32[]{:S(2)}) copy-start(f32[48,64]{1,0:T(8,128)} %param.15) | copy-start | bytes 36868
Sparse Core Ops, SparseCore 0:
  36.8 149.5 all-reduce.4
  189.2 831.5 all-reduce.2
where the time goes:
time: 1030 us
  waiting for transfers between devices  941 us (91%)
  between operations  45.4 us (4%)
  starting transfers between devices  15.4 us (1%)
  local copies, waits for them, and re-layouts  12.9 us (1%)
  matrix products  10.9 us (1%)
    psum x1, waiting for transfers between devices, per_device(): summed = lax.psum(factor_part, 'tm')  833 us
    psum x1, waiting for transfers between devices, per_device(): time_total = lax.psum(time_part, 'feeder')  107 us
  transfers between devices with their start and end apart: 8, of which 2 were waited for; matrix products, arithmetic and copies ran while one was open for 2% of the time, Pallas kernels for 0%

commit v1 on v0

v1 whole, which is shorter than its diff:
```python
import functools

import jax
import jax.numpy as jnp
from jax import lax
from jax.experimental import pallas as pl
from jax.experimental.pallas import tpu as pltpu
from jax.sharding import Mesh
from jax.sharding import PartitionSpec as P

LAGMAX = 1440
DATA_WEIGHT = 1.0 / 64.0
LAM_F = 0.1
LAM_X = 0.01
LAM_AR = 8.0
BETA_ONE = 0.9
BETA_TWO = 0.999
BIAS_FIRST = 1.0 - 0.9**8
BIAS_SECOND = 1.0 - 0.999**8
LEARNING_RATE = 0.05
ADAM_EPS = 1e-08

AXES = ("z_hi", "y", "z_lo", "x", "core")
FEEDER_AXES, TM_AXES, PLANE_AXES = AXES[:2], AXES[2:], AXES[3:]
PLANES, PLANE = 8, 8
TM = PLANES * PLANE
FEEDER = 8
SHARE = 48
BAND = 8
SPAN = 512
TILES = SPAN // 128
MAIN_ROWS = PLANES * SHARE // 2
ROWS = MAIN_ROWS + BAND * TILES
HOPS = 3
CHUNKS = (HOPS + 1) * TILES


def main_kernel(
    place, observed, words, factor, time, spread, shares, time_out, total, *, steps, planes
):
    step = pl.program_id(0)
    factor_half = factor[...].astype(jnp.bfloat16)
    time_half = time[...].astype(jnp.bfloat16)
    predicted = lax.dot_general(
        factor_half, time_half, (((0,), (0,)), ((), ())), preferred_element_type=jnp.float32
    )
    wide = lax.dot_general(
        words[...].astype(jnp.float32).astype(jnp.bfloat16),
        spread[...],
        (((0,), (0,)), ((), ())),
        preferred_element_type=jnp.float32,
    ).astype(jnp.int32)
    bit = jnp.left_shift(1, lax.broadcasted_iota(jnp.int32, wide.shape, 1) & 7)
    residual = jnp.where(
        (wide & bit) != 0, predicted - observed[...].astype(jnp.float32), 0.0
    ).astype(jnp.bfloat16)
    rows = DATA_WEIGHT * lax.dot_general(
        residual, time_half, (((1,), (1,)), ((), ())), preferred_element_type=jnp.float32
    )
    half = SHARE // 2
    for plane in range(planes):
        for local in range(PLANE):
            start = (plane * PLANE + local) * SHARE
            packed = jnp.concatenate(
                [rows[start : start + half], rows[start + half : start + SHARE]], axis=1
            )
            shares[local, pl.ds(pl.multiple_of((step * planes + plane) * half, 8), half)] = packed
    term = jnp.dot(factor_half, residual, preferred_element_type=jnp.float32)

    @pl.when(step == 0)
    def _():
        total[...] = term
        own = time[pl.ds(pl.multiple_of(place[0] * BAND, BAND), BAND), :]
        for tile in range(TILES):
            at = MAIN_ROWS + BAND * tile
            for local in range(PLANE):
                shares[local, at : at + BAND] = own[:, 128 * tile : 128 * tile + 128]

    @pl.when(step > 0)
    def _():
        total[...] = total[...] + term

    @pl.when(step == steps - 1)
    def _():
        for band in range(FEEDER):
            z, y = band >> 2, band & 3
            time_out[y, place[1] ^ z] = DATA_WEIGHT * total[BAND * band : BAND * band + BAND]


def main_terms(observed, words, factor, time, place, steps=4):
    feeders, span = observed.shape
    ranks, block = factor.shape[0], feeders // steps
    spread = (
        lax.broadcasted_iota(jnp.int32, (words.shape[0], span), 1) // 8
        == lax.broadcasted_iota(jnp.int32, (words.shape[0], span), 0)
    ).astype(jnp.bfloat16)
    return pl.pallas_call(
        functools.partial(main_kernel, steps=steps, planes=PLANES // steps),
        grid_spec=pltpu.PrefetchScalarGridSpec(
            num_scalar_prefetch=1,
            grid=(steps,),
            in_specs=[
                pl.BlockSpec((block, span), lambda s, place: (s, 0)),
                pl.BlockSpec((words.shape[0], block), lambda s, place: (0, s)),
                pl.BlockSpec((ranks, block), lambda s, place: (0, s)),
                pl.BlockSpec((ranks, span), lambda s, place: (0, 0)),
                pl.BlockSpec((words.shape[0], span), lambda s, place: (0, 0)),
            ],
            out_specs=[
                pl.BlockSpec((PLANE, ROWS, 128), lambda s, place: (0, 0, 0)),
                pl.BlockSpec((4, 2, BAND, span), lambda s, place: (0, 0, 0, 0)),
            ],
            scratch_shapes=[pltpu.VMEM((ranks, span), jnp.float32)],
        ),
        out_shape=[
            jax.ShapeDtypeStruct((PLANE, ROWS, 128), jnp.float32),
            jax.ShapeDtypeStruct((4, 2, BAND, span), jnp.float32),
        ],
        cost_estimate=pl.CostEstimate(flops=805306368, bytes_accessed=6_000_000, transcendentals=0),
        name="main_terms",
    )(place, observed, words, factor, time, spread)


def shifted_tiles(tiles, start, count, read):
    first, lane = start >> 7, start & 127
    back = (128 - lane) & 127
    rolled = [pltpu.roll(read(first + i), back, 1) for i in range(count + 1)]
    inside = lax.broadcasted_iota(jnp.int32, (BAND, 128), 1) < 128 - lane
    return [jnp.where(inside, rolled[i], rolled[i + 1]) for i in range(count)]


def ar_kernel(
    place, lags, weights, plane, beside, home, away, time_grad, spans, errors, weight_rows
):
    edge = HOPS * TILES
    for span in range(HOPS):
        for tile in range(TILES):
            value = beside[span, BAND * tile : BAND * tile + BAND]
            spans[span * TILES + tile] = value
            spans[edge + PLANE * TILES + span * TILES + tile] = value
    for span in range(PLANE):
        for tile in range(TILES):
            spans[edge + span * TILES + tile] = plane[span, BAND * tile : BAND * tile + BAND]
    weight_rows[...] = weights[...].T
    mine = weight_rows[pl.ds(pl.multiple_of(place[0] * BAND, BAND), BAND), :]
    own_tile = edge + place[3] * TILES
    own_column = own_tile * 128
    count = lags.shape[0]
    gains = [jnp.broadcast_to(mine[:, k : k + 1], (BAND, 128)) for k in range(count)]
    parts = [jnp.zeros((BAND, 128), jnp.float32) for _ in range(CHUNKS)]
    for k in range(count):
        moved = shifted_tiles(spans, own_column - lags[k], CHUNKS, lambda i: spans[i])
        parts = [part + gains[k] * tile for part, tile in zip(parts, moved)]
    lane = lax.broadcasted_iota(jnp.int32, (BAND, 128), 1)
    first = place[2] * SPAN
    for chunk in range(CHUNKS):
        column = first + 128 * chunk + lane
        inside = (column >= LAGMAX) & (column < TM * SPAN)
        errors[chunk] = jnp.where(inside, spans[own_tile + chunk] - parts[chunk], 0.0)
    errors[CHUNKS] = jnp.zeros((BAND, 128), jnp.float32)
    carried = [jnp.zeros((BAND, 128), jnp.float32) for _ in range(TILES)]
    for k in range(count):
        moved = shifted_tiles(errors, lags[k], TILES, lambda i: errors[i])
        carried = [part + gains[k] * tile for part, tile in zip(carried, moved)]
    for tile in range(TILES):
        at = slice(128 * tile, 128 * tile + 128)
        time_grad[:, at] = (
            home[:, at]
            + away[:, at]
            + LAM_AR * (errors[tile] - carried[tile])
            + LAM_X * spans[own_tile + tile]
        )


def ar_terms(place, lags, weights, plane, beside, home, away):
    in_vmem = pl.BlockSpec(memory_space=pltpu.VMEM)
    in_smem = pl.BlockSpec(memory_space=pltpu.SMEM)
    tiles = (2 * HOPS + PLANE) * TILES
    return pl.pallas_call(
        ar_kernel,
        in_specs=[in_smem, in_smem] + [in_vmem] * 5,
        out_specs=in_vmem,
        out_shape=jax.ShapeDtypeStruct((BAND, SPAN), jnp.float32),
        scratch_shapes=[
            pltpu.VMEM((tiles + 1, BAND, 128), jnp.float32),
            pltpu.VMEM((CHUNKS + 1, BAND, 128), jnp.float32),
            pltpu.VMEM(weights.shape[::-1], jnp.float32),
        ],
        cost_estimate=pl.CostEstimate(flops=2_000_000, bytes_accessed=400_000, transcendentals=0),
        compiler_params=pltpu.CompilerParams(vmem_limit_bytes=8 << 20),
        name="ar_terms",
    )(place, lags, weights, plane, beside, home, away)


def per_device(
    observed, mask_words, feeder_factor, time_factor, ar_weight, lags, moment_first, moment_second
):
    ranks = time_factor.shape[0]
    tm_place = lax.axis_index(TM_AXES)
    plane_place = lax.axis_index(PLANE_AXES)
    place = jnp.stack(
        [lax.axis_index(FEEDER_AXES), lax.axis_index("z_hi"), tm_place, plane_place]
    ).astype(jnp.int32)

    shares, time_part = main_terms(observed, mask_words.T, feeder_factor.T, time_factor, place)
    bands = lax.all_to_all(time_part, "y", 0, 0, tiled=True)
    got = lax.all_to_all(shares, PLANE_AXES, 0, 0, tiled=True)
    bands = bands.sum(0)
    away = lax.ppermute(bands[1], "z_hi", [(0, 1), (1, 0)])

    plane = got[:, MAIN_ROWS:]
    passed = jnp.where(plane_place < PLANE // 2, plane[PLANE - HOPS :], plane[:HOPS])
    pairs = [(t, t + PLANE) for t in range(TM - PLANE) if t % PLANE < PLANE // 2]
    pairs += [(t, t - PLANE) for t in range(PLANE, TM) if t % PLANE >= PLANE // 2]
    beside = lax.ppermute(passed, TM_AXES, pairs)
    planes = got[:, :MAIN_ROWS].sum(0).reshape(PLANES, SHARE // 2, 128)
    share = lax.all_to_all(planes, "z_lo", 0, 0, tiled=True).sum(0)
    time_grad = ar_terms(place, lags, ar_weight, plane, beside, bands[0], away)

    grad_share = jnp.concatenate([share[:, :ranks], share[:, ranks:]], axis=0)
    own_factor = lax.dynamic_slice_in_dim(feeder_factor, tm_place * SHARE, SHARE, 0)
    factor_grad = grad_share + LAM_F * own_factor
    new_first = BETA_ONE * moment_first + (1.0 - BETA_ONE) * factor_grad
    new_second = BETA_TWO * moment_second + (1.0 - BETA_TWO) * factor_grad * factor_grad
    update = (
        LEARNING_RATE * (new_first / BIAS_FIRST) / (jnp.sqrt(new_second / BIAS_SECOND) + ADAM_EPS)
    )
    return (own_factor - update, new_first, new_second, time_grad)


def solution(mesh):
    fine = Mesh(mesh.devices.reshape(2, 4, 8, 4, 2), AXES)
    rows = P(AXES, None)
    placed = (
        P(FEEDER_AXES, TM_AXES),
        P(FEEDER_AXES, TM_AXES),
        P(FEEDER_AXES, None),
        P(None, TM_AXES),
        P(),
        P(),
        rows,
        rows,
    )
    return jax.shard_map(
        per_device,
        mesh=fine,
        in_specs=placed,
        out_specs=(rows, rows, rows, P(FEEDER_AXES, TM_AXES)),
        check_vma=False,
    )
```

time: 1030 us -> 69.7 us (0.07)
  the two profiles are of different devices: /device:TPU:1 before, /device:TPU:32 now
where the time goes in v1:
time: 69.7 us; the launch traced here: 69.1 us
  starting transfers between devices  28.5 us (41%)
  waiting for transfers between devices  16.5 us (24%)
  blocking collectives  10.6 us (15%)
  Pallas kernels  9.11 us (13%)
  other arithmetic  2.58 us (4%)
  local copies, waits for them, and re-layouts  1.11 us (2%)
  between operations  0.74 us (1%)
    all_to_all x1, waiting for transfers between devices, per_device(): got = lax.all_to_all(shares, PLANE_AXES, 0, 0, tiled=True)  14.5 us
    all_to_all x1, starting transfers between devices, per_device(): share = lax.all_to_all(planes, 'z_lo', 0, 0, tiled=True).sum(0)  12.6 us
    all_to_all x1, blocking collectives, per_device(): bands = lax.all_to_all(time_part, 'y', 0, 0, tiled=True)  10.6 us
    ppermute x1, starting transfers between devices, per_device(): away = lax.ppermute(bands[1], 'z_hi', [(0, 1), (1, 0)])  8.2 us
    pallas_call x1, Pallas kernels, main_terms(): pl.pallas_call(functools.partial(main_kernel, steps=steps, planes=PLANES...  7.49 us
    all_to_all x1, starting transfers between devices, per_device(): got = lax.all_to_all(shares, PLANE_AXES, 0, 0, tiled=True)  4.3 us
    ppermute x1, starting transfers between devices, per_device(): beside = lax.ppermute(passed, TM_AXES, pairs)  3.37 us
    ppermute x1, waiting for transfers between devices, per_device(): away = lax.ppermute(bands[1], 'z_hi', [(0, 1), (1, 0)])  1.99 us
  transfers between devices with their start and end apart: 4, of which 2 were waited for; matrix products, arithmetic and copies ran while one was open for 2% of the time, Pallas kernels for 2%

profile of v1, /device:TPU:32, one launch (start us, length us, event | category | flops | bytes accessed | tf_op | source)
XLA Modules:
  0.0 69.1 jit_solution(17295554285422358285)
XLA Ops:
  0.7 0.6 fusion.spread
  1.3 0.6 pad_add_fusion.place
  1.9 7.5 %main_terms.1 = (f32[8,224,128]{2,1,0:T(8,128)}, f32[4,2,8,512]{3,2,1,0:T(8,128)}) custom-call(s32[4]{0:T(128)} %pad_add_fusion.place, bf16[3072,512]{1,0:T(8,128)(2,1)} %observed.1, s32[64,3072]{1,0:T(8,128)} %bitcast.12, f32[64,3072]{1,0:T(8,128)} %bitcast.11, f32[64,512]{1,0:T(8,128)} %time.1, bf16[64,512]{1,0:T(8,128)(2,1)} %fusion.spread), custom_call_target="tpu_custom_call" | custom-call | flops 805306368 | bytes 6000000 | tf_op jit(solution)/shard_map/main_terms/pallas_call | solution.py:97
  9.4 0.0 copy-start
  9.4 0.0 copy-start.1
  9.4 0.0 copy-start.2
  9.4 0.0 copy-start.3
  9.4 0.0 copy-start.4
  9.4 10.6 %all_to_all.15 = f32[4,2,8,512]{3,2,1,0:T(8,128)S(1)} all-to-all(f32[4,2,8,512]{3,2,1,0:T(8,128)} %get-tuple-element.7), channel_id=1, replica_groups=mesh['z_hi'=2,'y'=4,'z_lo'=8,'x'=4,'core'=2] {'y'}, dimensions={0} | all-to-all | bytes 262144 | tf_op jit(solution)/shard_map/all_to_all | solution.py:206
  20.0 4.3 %all-to-all-start = ((f32[8,224,128]{2,1,0:T(8,128)}), f32[8,224,128]{2,1,0:T(8,128)S(1)}, u32[]{:S(2)}, u32[]{:S(2)}) async-start(f32[8,224,128]{2,1,0:T(8,128)} %get-tuple-element.6), calls=%async_computation | async-start | bytes 1835008 | tf_op jit(solution)/shard_map/all_to_all | solution.py:207
  24.3 14.5 %all-to-all-done = f32[8,224,128]{2,1,0:T(8,128)S(1)} async-done(((f32[8,224,128]{2,1,0:T(8,128)}), f32[8,224,128]{2,1,0:T(8,128)S(1)}, u32[]{:S(2)}, u32[]{:S(2)}) %all-to-all-start) | async-done | bytes 917536 | tf_op jit(solution)/shard_map/all_to_all | solution.py:207
  38.8 0.7 slice_reduce_fusion
  39.5 12.6 %all-to-all-start.1 = ((f32[8,24,128]{2,1,0:T(8,128)}), f32[8,24,128]{2,1,0:T(8,128)S(1)}, u32[]{:S(2)}, u32[]{:S(2)}) async-start(f32[8,24,128]{2,1,0:T(8,128)} %bitcast.6), calls=%async_computation.1 | async-start | bytes 196608 | tf_op jit(solution)/shard_map/all_to_all | solution.py:217
  52.1 8.2 %collective-permute-start.1 = (f32[8,512]{1,0:T(8,128)S(1)}, f32[8,512]{1,0:T(8,128)S(1)}, u32[]{:S(2)}, u32[]{:S(2)}) collective-permute-start(f32[8,512]{1,0:T(8,128)S(1)} %get-tuple-element.11), channel_id=1, source_target_pairs={{0,256},{256,0},{1,257},{257,1},{2,258},{258,2},{3,259},{259,3},{4... | collective-permute-start | bytes 49160 | tf_op jit(solution)/shard_map/ppermute | solution.py:209
  60.4 3.4 %collective-permute-start = (f32[3,32,128]{2,1,0:T(8,128)S(1)}, f32[3,32,128]{2,1,0:T(8,128)S(1)}, u32[]{:S(2)}, u32[]{:S(2)}) collective-permute-start(f32[3,32,128]{2,1,0:T(8,128)S(1)} %slice_select_fusion), channel_id=1, source_target_pairs={{0,8},{1,9},{2,10},{3,11},{8,16},{9,17},{10,18},{11,19},{16,24},{1... | collective-permute-start | bytes 147464 | tf_op jit(solution)/shard_map/ppermute | solution.py:215
  63.7 0.9 %constant_dynamic-slice_fusion = f32[48,64]{0,1:T(8,128)S(1)} fusion(f32[3072,64]{0,1:T(8,128)} %param.10, s32[]{:T(128)S(6)} %select_n.16), kind=kLoop, calls=%fused_computation.19 | loop fusion | bytes 24580 | tf_op jit(solution)/shard_map/dynamic_slice | solution.py:221
  64.7 0.1 copy.14
  64.8 2.0 %collective-permute-done.1.away = f32[8,512]{1,0:T(8,128)S(1)} collective-permute-done((f32[8,512]{1,0:T(8,128)S(1)}, f32[8,512]{1,0:T(8,128)S(1)}, u32[]{:S(2)}, u32[]{:S(2)}) %collective-permute-start.1) | collective-permute-done | bytes 16416 | tf_op jit(solution)/shard_map/ppermute | solution.py:209
  66.8 0.0 collective-permute-done.beside
  66.8 0.0 copy-done
  66.8 0.0 copy-done.1
  66.8 0.0 copy-done.2
  66.8 1.6 %ar_terms.1 = f32[8,512]{1,0:T(8,128)} custom-call(s32[4]{0:T(128)S(1)} %copy-done.1, s32[10]{0:T(128)S(1)} %copy-done.2, f32[10,64]{1,0:T(8,128)S(1)} %copy-done, f32[8,32,128]{2,1,0:T(8,128)S(1)} %slice.37.plane, f32[3,32,128]{2,1,0:T(8,128)S(1)} %collective-permute-done.beside, f32[8,512]{1,0:T(8,128)S(1)} %get-tuple-element.12.home, ...), custom_call_target="tpu_custom_call" | custom-call | flops 2000000 | bytes 400000 | tf_op jit(solution)/shard_map/ar_terms/pallas_call | solution.py:179
  68.4 0.0 all-to-all-done.1
  68.4 0.1 fusion.6
  68.5 0.0 copy-done.3
  68.5 0.0 copy-done.4
  68.5 0.6 divide_subtract_fusion
  (7 shorter events, 0.1 us)
Async XLA Ops:
  9.4 57.4 %copy-start = (f32[10,64]{1,0:T(8,128)S(1)}, f32[10,64]{1,0:T(8,128)}, u32[]{:S(2)}) copy-start(f32[10,64]{1,0:T(8,128)} %weights.1) | copy-start | bytes 7684
  9.4 57.4 %copy-start.1 = (s32[4]{0:T(128)S(1)}, s32[4]{0:T(128)}, u32[]{:S(2)}) copy-start(s32[4]{0:T(128)} %pad_add_fusion.place) | copy-start | bytes 52
  9.4 57.4 %copy-start.2 = (s32[10]{0:T(128)S(1)}, s32[10]{0:T(128)}, u32[]{:S(2)}) copy-start(s32[10]{0:T(128)} %lags.1) | copy-start | bytes 124
  9.4 59.1 %copy-start.3 = (f32[48,64]{1,0:T(8,128)S(1)}, f32[48,64]{1,0:T(8,128)}, u32[]{:S(2)}) copy-start(f32[48,64]{1,0:T(8,128)} %param.14) | copy-start | bytes 36868
  9.4 59.1 %copy-start.4 = (f32[48,64]{1,0:T(8,128)S(1)}, f32[48,64]{1,0:T(8,128)}, u32[]{:S(2)}) copy-start(f32[48,64]{1,0:T(8,128)} %param.15) | copy-start | bytes 36868
  20.0 18.8 %all-to-all-start = ((f32[8,224,128]{2,1,0:T(8,128)}), f32[8,224,128]{2,1,0:T(8,128)S(1)}, u32[]{:S(2)}, u32[]{:S(2)}) async-start(f32[8,224,128]{2,1,0:T(8,128)} %get-tuple-element.6), calls=%async_computation | async-start | bytes 1835008 | tf_op jit(solution)/shard_map/all_to_all | solution.py:207
  39.5 28.9 %all-to-all-start.1 = ((f32[8,24,128]{2,1,0:T(8,128)}), f32[8,24,128]{2,1,0:T(8,128)S(1)}, u32[]{:S(2)}, u32[]{:S(2)}) async-start(f32[8,24,128]{2,1,0:T(8,128)} %bitcast.6), calls=%async_computation.1 | async-start | bytes 196608 | tf_op jit(solution)/shard_map/all_to_all | solution.py:217
  52.1 14.6 %collective-permute-start.1 = (f32[8,512]{1,0:T(8,128)S(1)}, f32[8,512]{1,0:T(8,128)S(1)}, u32[]{:S(2)}, u32[]{:S(2)}) collective-permute-start(f32[8,512]{1,0:T(8,128)S(1)} %get-tuple-element.11), channel_id=1, source_target_pairs={{0,256},{256,0},{1,257},{257,1},{2,258},{258,2},{3,259},{259,3},{4... | collective-permute-start | bytes 49160 | tf_op jit(solution)/shard_map/ppermute | solution.py:209
  60.4 6.4 %collective-permute-start = (f32[3,32,128]{2,1,0:T(8,128)S(1)}, f32[3,32,128]{2,1,0:T(8,128)S(1)}, u32[]{:S(2)}, u32[]{:S(2)}) collective-permute-start(f32[3,32,128]{2,1,0:T(8,128)S(1)} %slice_select_fusion), channel_id=1, source_target_pairs={{0,8},{1,9},{2,10},{3,11},{8,16},{9,17},{10,18},{11,19},{16,24},{1... | collective-permute-start | bytes 147464 | tf_op jit(solution)/shard_map/ppermute | solution.py:215

commit v2 on v1

v2 whole, which is shorter than its diff:
```python
import functools

import jax
import jax.numpy as jnp
from jax import lax
from jax.experimental import pallas as pl
from jax.experimental.pallas import tpu as pltpu
from jax.sharding import Mesh
from jax.sharding import PartitionSpec as P

LAGMAX = 1440
DATA_WEIGHT = 1.0 / 64.0
LAM_F = 0.1
LAM_X = 0.01
LAM_AR = 8.0
BETA_ONE = 0.9
BETA_TWO = 0.999
BIAS_FIRST = 1.0 - 0.9**8
BIAS_SECOND = 1.0 - 0.999**8
LEARNING_RATE = 0.05
ADAM_EPS = 1e-08

AXES = ("z_hi", "y", "z_lo", "x", "core")
FEEDER_AXES, TM_AXES = AXES[:2], AXES[2:]
PLANES, PLANE = 8, 8
TM = PLANES * PLANE
FEEDER = 8
SHARE = 48
BAND = 8
SPAN = 512
TILES = SPAN // 128
MAIN_ROWS = PLANES * SHARE // 2
BAND_ROWS = BAND * TILES
ROWS = MAIN_ROWS + 2 * BAND_ROWS
HOPS = 3
CHUNKS = (HOPS + 1) * TILES


def place_of(axes):
    place = 0
    for axis in axes:
        place = place * lax.axis_size(axis) + lax.axis_index(axis)
    return place


def main_kernel(observed, words, factor, time, keep, send, time_out, total, *, steps, planes):
    step = pl.program_id(0)
    factor_half = factor[...].astype(jnp.bfloat16)
    time_half = time[...].astype(jnp.bfloat16)
    predicted = lax.dot_general(
        factor_half, time_half, (((0,), (0,)), ((), ())), preferred_element_type=jnp.float32
    )
    word_count, span = words.shape[0], time.shape[1]
    spread = (
        lax.broadcasted_iota(jnp.int32, (word_count, span), 1) >> 3
        == lax.broadcasted_iota(jnp.int32, (word_count, span), 0)
    ).astype(jnp.float32).astype(jnp.bfloat16)
    wide = lax.dot_general(
        words[...].astype(jnp.float32).astype(jnp.bfloat16),
        spread,
        (((0,), (0,)), ((), ())),
        preferred_element_type=jnp.float32,
    ).astype(jnp.int32)
    bit = jnp.left_shift(1, lax.broadcasted_iota(jnp.int32, wide.shape, 1) & 7)
    residual = jnp.where(
        (wide & bit) != 0, predicted - observed[...].astype(jnp.float32), 0.0
    ).astype(jnp.bfloat16)
    rows = DATA_WEIGHT * lax.dot_general(
        residual, time_half, (((1,), (1,)), ((), ())), preferred_element_type=jnp.float32
    )
    half = SHARE // 2
    first = lax.axis_index("core") == 0
    for plane in range(planes):
        for x in range(PLANE // 2):
            pair = []
            for core in range(2):
                start = (plane * PLANE + 2 * x + core) * SHARE
                pair.append(
                    jnp.concatenate(
                        [rows[start : start + half], rows[start + half : start + SHARE]], axis=1
                    )
                )
            at = pl.ds(pl.multiple_of(x * MAIN_ROWS + (step * planes + plane) * half, 8), half)
            keep[at] = jnp.where(first, pair[0], pair[1])
            send[at] = jnp.where(first, pair[1], pair[0])
    term = jnp.dot(factor_half, residual, preferred_element_type=jnp.float32)

    @pl.when(step == 0)
    def _():
        total[...] = term
        own = time[pl.ds(pl.multiple_of(place_of(FEEDER_AXES) * BAND, BAND), BAND), :]
        for tile in range(TILES):
            at = PLANE // 2 * MAIN_ROWS + BAND * tile
            keep[at : at + BAND] = own[:, 128 * tile : 128 * tile + 128]
            send[at : at + BAND] = own[:, 128 * tile : 128 * tile + 128]

    @pl.when(step > 0)
    def _():
        total[...] = total[...] + term

    @pl.when(step == steps - 1)
    def _():
        z_hi = lax.axis_index("z_hi")
        for band in range(FEEDER):
            z, y = band >> 2, band & 3
            time_out[y, z_hi ^ z] = DATA_WEIGHT * total[BAND * band : BAND * band + BAND]


def main_terms(observed, words, factor, time, steps=4):
    feeders, span = observed.shape
    ranks, block = factor.shape[0], feeders // steps
    half_rows = PLANE // 2 * MAIN_ROWS + BAND_ROWS
    return pl.pallas_call(
        functools.partial(main_kernel, steps=steps, planes=PLANES // steps),
        grid=(steps,),
        in_specs=[
            pl.BlockSpec((block, span), lambda s: (s, 0)),
            pl.BlockSpec((words.shape[0], block), lambda s: (0, s)),
            pl.BlockSpec((ranks, block), lambda s: (0, s)),
            pl.BlockSpec((ranks, span), lambda s: (0, 0)),
        ],
        out_specs=[
            pl.BlockSpec((half_rows, 128), lambda s: (0, 0)),
            pl.BlockSpec((half_rows, 128), lambda s: (0, 0)),
            pl.BlockSpec((4, 2, BAND, span), lambda s: (0, 0, 0, 0)),
        ],
        scratch_shapes=[pltpu.VMEM((ranks, span), jnp.float32)],
        out_shape=[
            jax.ShapeDtypeStruct((half_rows, 128), jnp.float32),
            jax.ShapeDtypeStruct((half_rows, 128), jnp.float32),
            jax.ShapeDtypeStruct((4, 2, BAND, span), jnp.float32),
        ],
        cost_estimate=pl.CostEstimate(flops=805306368, bytes_accessed=6_000_000, transcendentals=0),
        compiler_params=pltpu.CompilerParams(vmem_limit_bytes=24 << 20),
        name="main_terms",
    )(*(pltpu.with_memory_space_constraint(a, pltpu.HBM) for a in (observed, words, factor, time)))


def pair_kernel(keep, got, out):
    first = lax.axis_index("core") == 0
    tail = PLANE // 2 * MAIN_ROWS
    mine, other = keep[tail:], got[tail:]
    for x in range(PLANE // 2):
        at = slice(x * MAIN_ROWS, (x + 1) * MAIN_ROWS)
        out[x, :MAIN_ROWS] = keep[at] + got[at]
        out[x, MAIN_ROWS : MAIN_ROWS + BAND_ROWS] = jnp.where(first, mine, other)
        out[x, MAIN_ROWS + BAND_ROWS :] = jnp.where(first, other, mine)


def pair_terms(keep, got):
    in_vmem = pl.BlockSpec(memory_space=pltpu.VMEM)
    return pl.pallas_call(
        pair_kernel,
        in_specs=[in_vmem, in_vmem],
        out_specs=in_vmem,
        out_shape=jax.ShapeDtypeStruct((PLANE // 2, ROWS, 128), jnp.float32),
        cost_estimate=pl.CostEstimate(flops=100_000, bytes_accessed=1_400_000, transcendentals=0),
        compiler_params=pltpu.CompilerParams(vmem_limit_bytes=8 << 20),
        name="pair_terms",
    )(keep, got)


def split_kernel(got, planes, passed):
    total = got[0, :MAIN_ROWS]
    for x in range(1, PLANE // 2):
        total = total + got[x, :MAIN_ROWS]
    half = SHARE // 2
    for z in range(PLANES):
        planes[z] = total[half * z : half * z + half]
    late = place_of(AXES[3:]) < PLANE // 2
    for span in range(HOPS):
        ends = []
        for source in (PLANE - HOPS + span, span):
            at = MAIN_ROWS + BAND_ROWS * (source & 1)
            ends.append(got[source >> 1, at : at + BAND_ROWS])
        passed[span] = jnp.where(late, ends[0], ends[1])


def split_terms(got):
    in_vmem = pl.BlockSpec(memory_space=pltpu.VMEM)
    return pl.pallas_call(
        split_kernel,
        in_specs=[in_vmem],
        out_specs=[in_vmem, in_vmem],
        out_shape=[
            jax.ShapeDtypeStruct((PLANES, SHARE // 2, 128), jnp.float32),
            jax.ShapeDtypeStruct((HOPS, BAND_ROWS, 128), jnp.float32),
        ],
        cost_estimate=pl.CostEstimate(flops=100_000, bytes_accessed=700_000, transcendentals=0),
        compiler_params=pltpu.CompilerParams(vmem_limit_bytes=8 << 20),
        name="split_terms",
    )(got)


def shifted_tiles(start, count, read):
    first, lane = start >> 7, start & 127
    back = (128 - lane) & 127
    rolled = [pltpu.roll(read(first + i), back, 1) for i in range(count + 1)]
    inside = lax.broadcasted_iota(jnp.int32, (BAND, 128), 1) < 128 - lane
    return [jnp.where(inside, rolled[i], rolled[i + 1]) for i in range(count)]


def ar_kernel(
    lags, weights, plane, beside, home, away, time_grad, spans, errors, weight_rows
):
    edge = HOPS * TILES
    for span in range(HOPS):
        for tile in range(TILES):
            value = beside[span, BAND * tile : BAND * tile + BAND]
            spans[span * TILES + tile] = value
            spans[edge + PLANE * TILES + span * TILES + tile] = value
    for span in range(PLANE):
        for tile in range(TILES):
            spans[edge + span * TILES + tile] = plane[span, BAND * tile : BAND * tile + BAND]
    weight_rows[...] = weights[...].T
    mine = weight_rows[pl.ds(pl.multiple_of(place_of(FEEDER_AXES) * BAND, BAND), BAND), :]
    own_tile = edge + place_of(AXES[3:]) * TILES
    own_column = own_tile * 128
    count = lags.shape[0]
    gains = [jnp.broadcast_to(mine[:, k : k + 1], (BAND, 128)) for k in range(count)]
    parts = [jnp.zeros((BAND, 128), jnp.float32) for _ in range(CHUNKS)]
    for k in range(count):
        moved = shifted_tiles(own_column - lags[k], CHUNKS, lambda i: spans[i])
        parts = [part + gains[k] * tile for part, tile in zip(parts, moved)]
    lane = lax.broadcasted_iota(jnp.int32, (BAND, 128), 1)
    first = place_of(TM_AXES) * SPAN
    for chunk in range(CHUNKS):
        column = first + 128 * chunk + lane
        inside = (column >= LAGMAX) & (column < TM * SPAN)
        errors[chunk] = jnp.where(inside, spans[own_tile + chunk] - parts[chunk], 0.0)
    errors[CHUNKS] = jnp.zeros((BAND, 128), jnp.float32)
    carried = [jnp.zeros((BAND, 128), jnp.float32) for _ in range(TILES)]
    for k in range(count):
        moved = shifted_tiles(lags[k], TILES, lambda i: errors[i])
        carried = [part + gains[k] * tile for part, tile in zip(carried, moved)]
    for tile in range(TILES):
        at = slice(128 * tile, 128 * tile + 128)
        time_grad[:, at] = (
            home[:, at]
            + away[:, at]
            + LAM_AR * (errors[tile] - carried[tile])
            + LAM_X * spans[own_tile + tile]
        )


def ar_terms(lags, weights, plane, beside, home, away):
    in_vmem = pl.BlockSpec(memory_space=pltpu.VMEM)
    in_smem = pl.BlockSpec(memory_space=pltpu.SMEM)
    tiles = (2 * HOPS + PLANE) * TILES
    return pl.pallas_call(
        ar_kernel,
        in_specs=[in_smem] + [in_vmem] * 5,
        out_specs=in_vmem,
        out_shape=jax.ShapeDtypeStruct((BAND, SPAN), jnp.float32),
        scratch_shapes=[
            pltpu.VMEM((tiles + 1, BAND, 128), jnp.float32),
            pltpu.VMEM((CHUNKS + 1, BAND, 128), jnp.float32),
            pltpu.VMEM(weights.shape[::-1], jnp.float32),
        ],
        cost_estimate=pl.CostEstimate(flops=2_000_000, bytes_accessed=400_000, transcendentals=0),
        compiler_params=pltpu.CompilerParams(vmem_limit_bytes=8 << 20),
        name="ar_terms",
    )(lags, weights, plane, beside, home, away)


def per_device(
    observed, mask_words, feeder_factor, time_factor, ar_weight, lags, moment_first, moment_second
):
    ranks = time_factor.shape[0]
    tm_place = lax.axis_index(TM_AXES)

    keep, send, time_part = main_terms(observed, mask_words.T, feeder_factor.T, time_factor)
    got = lax.ppermute(send, "core", [(0, 1), (1, 0)])
    bands = lax.all_to_all(time_part, "y", 0, 0, tiled=True)
    got = lax.all_to_all(pair_terms(keep, got), "x", 0, 0, tiled=True)
    bands = bands.sum(0)
    away = lax.ppermute(bands[1], "z_hi", [(0, 1), (1, 0)])

    planes, passed = split_terms(got)
    plane = got[:, MAIN_ROWS:].reshape(PLANE, BAND_ROWS, 128)
    pairs = [(t, t + PLANE) for t in range(TM - PLANE) if t % PLANE < PLANE // 2]
    pairs += [(t, t - PLANE) for t in range(PLANE, TM) if t % PLANE >= PLANE // 2]
    beside = lax.ppermute(passed, TM_AXES, pairs)
    share = lax.all_to_all(planes, "z_lo", 0, 0, tiled=True)
    share = share.sum(0)
    time_grad = ar_terms(lags, ar_weight, plane, beside, bands[0], away)

    grad_share = jnp.concatenate([share[:, :ranks], share[:, ranks:]], axis=0)
    own_factor = lax.dynamic_slice_in_dim(feeder_factor, tm_place * SHARE, SHARE, 0)
    factor_grad = grad_share + LAM_F * own_factor
    new_first = BETA_ONE * moment_first + (1.0 - BETA_ONE) * factor_grad
    new_second = BETA_TWO * moment_second + (1.0 - BETA_TWO) * factor_grad * factor_grad
    update = (
        LEARNING_RATE * (new_first / BIAS_FIRST) / (jnp.sqrt(new_second / BIAS_SECOND) + ADAM_EPS)
    )
    return (own_factor - update, new_first, new_second, time_grad)


def solution(mesh):
    fine = Mesh(mesh.devices.reshape(2, 4, 8, 4, 2), AXES)
    rows = P(AXES, None)
    placed = (
        P(FEEDER_AXES, TM_AXES),
        P(FEEDER_AXES, TM_AXES),
        P(FEEDER_AXES, None),
        P(None, TM_AXES),
        P(),
        P(),
        rows,
        rows,
    )
    return jax.shard_map(
        per_device,
        mesh=fine,
        in_specs=placed,
        out_specs=(rows, rows, rows, P(FEEDER_AXES, TM_AXES)),
        check_vma=False,
    )
```

time: 69.7 us -> 65.3 us (0.937)
  waiting for transfers between devices: 16.5 us -> 8.83 us
  blocking collectives: 10.6 us -> 13.9 us
  starting transfers between devices: 28.5 us -> 30.7 us
  other arithmetic: 2.58 us -> 0.67 us
    all_to_all x2, waiting for transfers between devices: 14.5 us -> 5.31 us  [the longest x1 5.31 us: per_device(): bands = lax.all_to_all(time_part, 'y', 0, 0, tiled=True)]
    all_to_all x1, blocking collectives: 10.6 us -> 13.9 us  [per_device(): got = lax.all_to_all(pair_terms(keep, got), 'x', 0, 0, tiled=True)]
    ppermute x0 -> x1, starting transfers between devices: none -> 2.05 us  [per_device(): got = lax.ppermute(send, 'core', [(0, 1), (1, 0)])]
    ppermute x0 -> x1, waiting for transfers between devices: none -> 1.71 us  [per_device(): got = lax.ppermute(send, 'core', [(0, 1), (1, 0)])]
    pallas_call x1, Pallas kernels: 7.49 us -> 6.48 us  [main_terms(): pl.pallas_call(functools.partial(main_kernel, steps=steps, planes=PLANES...]
    pallas_call x1 -> x3, Pallas kernels: 1.62 us -> 2.33 us  [the longest x1 1.62 us: ar_terms(): pl.pallas_call(ar_kernel, in_specs=[in_smem] + [in_vmem] * 5, out_specs=i...]
  transfers between devices with their start and end apart: 4 -> 5, of which waited for: 2 -> 3; matrix products, arithmetic and copies ran while one was open for 2% -> 2% of each run, Pallas kernels for 2% -> 4%
where the time goes in v2:
time: 65.3 us; the launch traced here: 64.7 us
  starting transfers between devices  30.7 us (47%)
  blocking collectives  13.9 us (21%)
  waiting for transfers between devices  8.83 us (14%)
  Pallas kernels  8.81 us (13%)
  local copies, waits for them, and re-layouts  1.11 us (2%)
  between operations  0.71 us (1%)
  other arithmetic  0.67 us (1%)
    all_to_all x1, blocking collectives, per_device(): got = lax.all_to_all(pair_terms(keep, got), 'x', 0, 0, tiled=True)  13.9 us
    all_to_all x1, starting transfers between devices, per_device(): share = lax.all_to_all(planes, 'z_lo', 0, 0, tiled=True)  12.6 us
    ppermute x1, starting transfers between devices, per_device(): away = lax.ppermute(bands[1], 'z_hi', [(0, 1), (1, 0)])  8.22 us
    pallas_call x1, Pallas kernels, main_terms(): pl.pallas_call(functools.partial(main_kernel, steps=steps, planes=PLANES...  6.48 us
    all_to_all x1, waiting for transfers between devices, per_device(): bands = lax.all_to_all(time_part, 'y', 0, 0, tiled=True)  5.31 us
    all_to_all x1, starting transfers between devices, per_device(): bands = lax.all_to_all(time_part, 'y', 0, 0, tiled=True)  4.47 us
    ppermute x1, starting transfers between devices, per_device(): beside = lax.ppermute(passed, TM_AXES, pairs)  3.37 us
    ppermute x1, starting transfers between devices, per_device(): got = lax.ppermute(send, 'core', [(0, 1), (1, 0)])  2.05 us
  transfers between devices with their start and end apart: 5, of which 3 were waited for; matrix products, arithmetic and copies ran while one was open for 2% of the time, Pallas kernels for 4%

profile of v2, /device:TPU:32, one launch (start us, length us, event | category | flops | bytes accessed | tf_op | source)
XLA Modules:
  0.0 64.7 jit_solution(958406601673977392)
XLA Ops:
  0.6 6.5 %main_terms.1 = (f32[800,128]{1,0:T(8,128)S(1)}, f32[800,128]{1,0:T(8,128)S(1)}, f32[4,2,8,512]{3,2,1,0:T(8,128)}) custom-call(bf16[3072,512]{1,0:T(8,128)(2,1)} %observed.1, s32[64,3072]{1,0:T(8,128)} %bitcast.9, f32[64,3072]{1,0:T(8,128)} %bitcast.8, f32[64,512]{1,0:T(8,128)} %time.1), custom_call_target="tpu_custom_call" | custom-call | flops 805306368 | bytes 6000000 | tf_op jit(solution)/shard_map/main_terms/pallas_call | solution.py:113
  7.1 0.0 copy-start
  7.1 0.0 copy-start.1
  7.1 0.0 copy-start.2
  7.1 0.0 copy-start.3
  7.1 2.1 %collective-permute-start = (f32[800,128]{1,0:T(8,128)S(1)}, f32[800,128]{1,0:T(8,128)S(1)}, u32[]{:S(2)}, u32[]{:S(2)}) collective-permute-start(f32[800,128]{1,0:T(8,128)S(1)} %get-tuple-element.10), channel_id=1, source_target_pairs={{0,1},{1,0},{2,3},{3,2},{4,5},{5,4},{6,7},{7,6},{8,9},{9,8},{10,11... | collective-permute-start | bytes 1228808 | tf_op jit(solution)/shard_map/ppermute | solution.py:273
  9.2 1.7 %collective-permute-done.got = f32[800,128]{1,0:T(8,128)S(1)} collective-permute-done((f32[800,128]{1,0:T(8,128)S(1)}, f32[800,128]{1,0:T(8,128)S(1)}, u32[]{:S(2)}, u32[]{:S(2)}) %collective-permute-start) | collective-permute-done | bytes 409632 | tf_op jit(solution)/shard_map/ppermute | solution.py:273
  11.0 13.9 %all_to_all.15.got = f32[4,256,128]{2,1,0:T(8,128)S(1)} all-to-all(f32[4,256,128]{2,1,0:T(8,128)S(1)} %pair_terms.1), channel_id=1, replica_groups=mesh['z_hi'=2,'y'=4,'z_lo'=8,'x'=4,'core'=2] {'x'}, dimensions={0} | all-to-all | bytes 1048576 | tf_op jit(solution)/shard_map/all_to_all | solution.py:275
  24.8 4.5 %all-to-all-start.2 = ((f32[4,2,8,512]{3,2,1,0:T(8,128)}), f32[4,2,8,512]{3,2,1,0:T(8,128)S(1)}, u32[]{:S(2)}, u32[]{:S(2)}) async-start(f32[4,2,8,512]{3,2,1,0:T(8,128)} %get-tuple-element.13), calls=%async_computation.2 | async-start | bytes 262144 | tf_op jit(solution)/shard_map/all_to_all | solution.py:274
  29.3 0.7 %split_terms.1 = (f32[8,24,128]{2,1,0:T(8,128)}, f32[3,32,128]{2,1,0:T(8,128)S(1)}) custom-call(f32[4,256,128]{2,1,0:T(8,128)S(1)} %all_to_all.15.got), custom_call_target="tpu_custom_call" | custom-call | flops 100000 | bytes 700000 | tf_op jit(solution)/shard_map/split_terms/pallas_call | solution.py:181
  30.0 5.3 %all-to-all-done.2 = f32[4,2,8,512]{3,2,1,0:T(8,128)S(1)} async-done(((f32[4,2,8,512]{3,2,1,0:T(8,128)}), f32[4,2,8,512]{3,2,1,0:T(8,128)S(1)}, u32[]{:S(2)}, u32[]{:S(2)}) %all-to-all-start.2) | async-done | bytes 131104 | tf_op jit(solution)/shard_map/all_to_all | solution.py:274
  35.3 12.6 %all-to-all-start.1 = ((f32[8,24,128]{2,1,0:T(8,128)}), f32[8,24,128]{2,1,0:T(8,128)S(1)}, u32[]{:S(2)}, u32[]{:S(2)}) async-start(f32[8,24,128]{2,1,0:T(8,128)} %get-tuple-element.11), calls=%async_computation.1 | async-start | bytes 196608 | tf_op jit(solution)/shard_map/all_to_all | solution.py:284
  47.9 8.2 %collective-permute-start.2 = (f32[8,512]{1,0:T(8,128)S(1)}, f32[8,512]{1,0:T(8,128)S(1)}, u32[]{:S(2)}, u32[]{:S(2)}) collective-permute-start(f32[8,512]{1,0:T(8,128)S(1)} %get-tuple-element.17), channel_id=1, source_target_pairs={{0,256},{256,0},{1,257},{257,1},{2,258},{258,2},{3,259},{259,3},{4... | collective-permute-start | bytes 49160 | tf_op jit(solution)/shard_map/ppermute | solution.py:277
  56.2 3.4 %collective-permute-start.1 = (f32[3,32,128]{2,1,0:T(8,128)S(1)}, f32[3,32,128]{2,1,0:T(8,128)S(1)}, u32[]{:S(2)}, u32[]{:S(2)}) collective-permute-start(f32[3,32,128]{2,1,0:T(8,128)S(1)} %get-tuple-element.12), channel_id=1, source_target_pairs={{0,8},{1,9},{2,10},{3,11},{8,16},{9,17},{10,18},{11,19},{16,24},{1... | collective-permute-start | bytes 147464 | tf_op jit(solution)/shard_map/ppermute | solution.py:283
  59.5 0.9 %constant_dynamic-slice_fusion = f32[48,64]{0,1:T(8,128)S(1)} fusion(f32[3072,64]{0,1:T(8,128)} %param.10, s32[]{:T(128)S(6)} %select_n.3), kind=kLoop, calls=%fused_computation.7 | loop fusion | bytes 24580 | tf_op jit(solution)/shard_map/dynamic_slice | solution.py:289
  60.5 0.1 copy.13
  60.6 1.8 %collective-permute-done.2.away = f32[8,512]{1,0:T(8,128)S(1)} collective-permute-done((f32[8,512]{1,0:T(8,128)S(1)}, f32[8,512]{1,0:T(8,128)S(1)}, u32[]{:S(2)}, u32[]{:S(2)}) %collective-permute-start.2) | collective-permute-done | bytes 16416 | tf_op jit(solution)/shard_map/ppermute | solution.py:277
  62.4 0.0 collective-permute-done.1.beside
  62.4 0.0 copy-done
  62.4 0.0 copy-done.1
  62.4 1.6 %ar_terms.1 = f32[8,512]{1,0:T(8,128)} custom-call(s32[10]{0:T(128)S(1)} %copy-done.1, f32[10,64]{1,0:T(8,128)S(1)} %copy-done, f32[8,32,128]{2,1,0:T(8,128)S(1)} %bitcast.7, f32[3,32,128]{2,1,0:T(8,128)S(1)} %collective-permute-done.1.beside, f32[8,512]{1,0:T(8,128)S(1)} %get-tuple-element.18.home, f32[8,512]{1,0:T(8,128)S(1)} %collective-permute-done.2.away), custom_call_target="tpu_custom_call" | custom-call | flops 2000000 | bytes 400000 | tf_op jit(solution)/shard_map/ar_terms/pallas_call | solution.py:250
  64.0 0.0 all-to-all-done.1
  64.0 0.1 fusion.2
  64.1 0.0 copy-done.2
  64.1 0.0 copy-done.3
  64.1 0.6 divide_subtract_fusion
  (5 shorter events, 0.1 us)
Async XLA Ops:
  7.1 55.3 %copy-start = (f32[10,64]{1,0:T(8,128)S(1)}, f32[10,64]{1,0:T(8,128)}, u32[]{:S(2)}) copy-start(f32[10,64]{1,0:T(8,128)} %weights.1) | copy-start | bytes 7684
  7.1 55.3 %copy-start.1 = (s32[10]{0:T(128)S(1)}, s32[10]{0:T(128)}, u32[]{:S(2)}) copy-start(s32[10]{0:T(128)} %lags.1) | copy-start | bytes 124
  7.1 57.0 %copy-start.2 = (f32[48,64]{1,0:T(8,128)S(1)}, f32[48,64]{1,0:T(8,128)}, u32[]{:S(2)}) copy-start(f32[48,64]{1,0:T(8,128)} %param.14) | copy-start | bytes 36868
  7.1 57.0 %copy-start.3 = (f32[48,64]{1,0:T(8,128)S(1)}, f32[48,64]{1,0:T(8,128)}, u32[]{:S(2)}) copy-start(f32[48,64]{1,0:T(8,128)} %param.15) | copy-start | bytes 36868
  7.1 3.8 %collective-permute-start = (f32[800,128]{1,0:T(8,128)S(1)}, f32[800,128]{1,0:T(8,128)S(1)}, u32[]{:S(2)}, u32[]{:S(2)}) collective-permute-start(f32[800,128]{1,0:T(8,128)S(1)} %get-tuple-element.10), channel_id=1, source_target_pairs={{0,1},{1,0},{2,3},{3,2},{4,5},{5,4},{6,7},{7,6},{8,9},{9,8},{10,11... | collective-permute-start | bytes 1228808 | tf_op jit(solution)/shard_map/ppermute | solution.py:273
  24.8 10.4 %all-to-all-start.2 = ((f32[4,2,8,512]{3,2,1,0:T(8,128)}), f32[4,2,8,512]{3,2,1,0:T(8,128)S(1)}, u32[]{:S(2)}, u32[]{:S(2)}) async-start(f32[4,2,8,512]{3,2,1,0:T(8,128)} %get-tuple-element.13), calls=%async_computation.2 | async-start | bytes 262144 | tf_op jit(solution)/shard_map/all_to_all | solution.py:274
  35.3 28.7 %all-to-all-start.1 = ((f32[8,24,128]{2,1,0:T(8,128)}), f32[8,24,128]{2,1,0:T(8,128)S(1)}, u32[]{:S(2)}, u32[]{:S(2)}) async-start(f32[8,24,128]{2,1,0:T(8,128)} %get-tuple-element.11), calls=%async_computation.1 | async-start | bytes 196608 | tf_op jit(solution)/shard_map/all_to_all | solution.py:284
  47.9 14.4 %collective-permute-start.2 = (f32[8,512]{1,0:T(8,128)S(1)}, f32[8,512]{1,0:T(8,128)S(1)}, u32[]{:S(2)}, u32[]{:S(2)}) collective-permute-start(f32[8,512]{1,0:T(8,128)S(1)} %get-tuple-element.17), channel_id=1, source_target_pairs={{0,256},{256,0},{1,257},{257,1},{2,258},{258,2},{3,259},{259,3},{4... | collective-permute-start | bytes 49160 | tf_op jit(solution)/shard_map/ppermute | solution.py:277
  56.2 6.2 %collective-permute-start.1 = (f32[3,32,128]{2,1,0:T(8,128)S(1)}, f32[3,32,128]{2,1,0:T(8,128)S(1)}, u32[]{:S(2)}, u32[]{:S(2)}) collective-permute-start(f32[3,32,128]{2,1,0:T(8,128)S(1)} %get-tuple-element.12), channel_id=1, source_target_pairs={{0,8},{1,9},{2,10},{3,11},{8,16},{9,17},{10,18},{11,19},{16,24},{1... | collective-permute-start | bytes 147464 | tf_op jit(solution)/shard_map/ppermute | solution.py:283

commit v3 on v2

--- a/solution.py
+++ b/solution.py
@@ -54,16 +54,17 @@
     spread = (
         lax.broadcasted_iota(jnp.int32, (word_count, span), 1) >> 3
         == lax.broadcasted_iota(jnp.int32, (word_count, span), 0)
-    ).astype(jnp.float32).astype(jnp.bfloat16)
+    )
+    power = 1.0 / jnp.left_shift(2, lax.broadcasted_iota(jnp.int32, (1, span), 1) & 7).astype(jnp.float32)
+    spread = jnp.where(spread, power, 0.0).astype(jnp.bfloat16)
     wide = lax.dot_general(
         words[...].astype(jnp.float32).astype(jnp.bfloat16),
         spread,
         (((0,), (0,)), ((), ())),
         preferred_element_type=jnp.float32,
-    ).astype(jnp.int32)
-    bit = jnp.left_shift(1, lax.broadcasted_iota(jnp.int32, wide.shape, 1) & 7)
+    )
     residual = jnp.where(
-        (wide & bit) != 0, predicted - observed[...].astype(jnp.float32), 0.0
+        wide - jnp.floor(wide) >= 0.5, predicted - observed[...].astype(jnp.float32), 0.0
     ).astype(jnp.bfloat16)
     rows = DATA_WEIGHT * lax.dot_general(
         residual, time_half, (((1,), (1,)), ((), ())), preferred_element_type=jnp.float32
@@ -271,6 +272,7 @@
 
     keep, send, time_part = main_terms(observed, mask_words.T, feeder_factor.T, time_factor)
     got = lax.ppermute(send, "core", [(0, 1), (1, 0)])
+    own_factor = lax.dynamic_slice_in_dim(feeder_factor, tm_place * SHARE, SHARE, 0)
     bands = lax.all_to_all(time_part, "y", 0, 0, tiled=True)
     got = lax.all_to_all(pair_terms(keep, got), "x", 0, 0, tiled=True)
     bands = bands.sum(0)
@@ -286,7 +288,6 @@
     time_grad = ar_terms(lags, ar_weight, plane, beside, bands[0], away)
 
     grad_share = jnp.concatenate([share[:, :ranks], share[:, ranks:]], axis=0)
-    own_factor = lax.dynamic_slice_in_dim(feeder_factor, tm_place * SHARE, SHARE, 0)
     factor_grad = grad_share + LAM_F * own_factor
     new_first = BETA_ONE * moment_first + (1.0 - BETA_ONE) * factor_grad
     new_second = BETA_TWO * moment_second + (1.0 - BETA_TWO) * factor_grad * factor_grad

time: 65.3 us -> 65.2 us (level)
  no operation moved by 1% of the time
where the time goes in v3:
time: 65.2 us; the launch traced here: 64.6 us
  starting transfers between devices  30.7 us (47%)
  blocking collectives  13.9 us (21%)
  waiting for transfers between devices  8.83 us (14%)
  Pallas kernels  8.69 us (13%)
  local copies, waits for them, and re-layouts  1.11 us (2%)
  between operations  0.71 us (1%)
  other arithmetic  0.67 us (1%)
    all_to_all x1, blocking collectives, per_device(): got = lax.all_to_all(pair_terms(keep, got), 'x', 0, 0, tiled=True)  13.9 us
    all_to_all x1, starting transfers between devices, per_device(): share = lax.all_to_all(planes, 'z_lo', 0, 0, tiled=True)  12.6 us
    ppermute x1, starting transfers between devices, per_device(): away = lax.ppermute(bands[1], 'z_hi', [(0, 1), (1, 0)])  8.22 us
    pallas_call x1, Pallas kernels, main_terms(): pl.pallas_call(functools.partial(main_kernel, steps=steps, planes=PLANES...  6.35 us
    all_to_all x1, waiting for transfers between devices, per_device(): bands = lax.all_to_all(time_part, 'y', 0, 0, tiled=True)  5.31 us
    all_to_all x1, starting transfers between devices, per_device(): bands = lax.all_to_all(time_part, 'y', 0, 0, tiled=True)  4.47 us
    ppermute x1, starting transfers between devices, per_device(): beside = lax.ppermute(passed, TM_AXES, pairs)  3.37 us
    ppermute x1, starting transfers between devices, per_device(): got = lax.ppermute(send, 'core', [(0, 1), (1, 0)])  2.05 us
  transfers between devices with their start and end apart: 5, of which 3 were waited for; matrix products, arithmetic and copies ran while one was open for 2% of the time, Pallas kernels for 4%

profile of v3, /device:TPU:32, one launch (start us, length us, event | category | flops | bytes accessed | tf_op | source)
XLA Modules:
  0.0 64.6 jit_solution(6435624937984571275)
XLA Ops:
  0.6 6.4 %main_terms.1 = (f32[800,128]{1,0:T(8,128)S(1)}, f32[800,128]{1,0:T(8,128)S(1)}, f32[4,2,8,512]{3,2,1,0:T(8,128)}) custom-call(bf16[3072,512]{1,0:T(8,128)(2,1)} %observed.1, s32[64,3072]{1,0:T(8,128)} %bitcast.9, f32[64,3072]{1,0:T(8,128)} %bitcast.8, f32[64,512]{1,0:T(8,128)} %time.1), custom_call_target="tpu_custom_call" | custom-call | flops 805306368 | bytes 6000000 | tf_op jit(solution)/shard_map/main_terms/pallas_call | solution.py:114
  7.0 0.0 copy-start
  7.0 0.0 copy-start.1
  7.0 0.0 copy-start.2
  7.0 0.0 copy-start.3
  7.0 2.1 %collective-permute-start = (f32[800,128]{1,0:T(8,128)S(1)}, f32[800,128]{1,0:T(8,128)S(1)}, u32[]{:S(2)}, u32[]{:S(2)}) collective-permute-start(f32[800,128]{1,0:T(8,128)S(1)} %get-tuple-element.10), channel_id=1, source_target_pairs={{0,1},{1,0},{2,3},{3,2},{4,5},{5,4},{6,7},{7,6},{8,9},{9,8},{10,11... | collective-permute-start | bytes 1228808 | tf_op jit(solution)/shard_map/ppermute | solution.py:274
  9.1 1.7 %collective-permute-done.got = f32[800,128]{1,0:T(8,128)S(1)} collective-permute-done((f32[800,128]{1,0:T(8,128)S(1)}, f32[800,128]{1,0:T(8,128)S(1)}, u32[]{:S(2)}, u32[]{:S(2)}) %collective-permute-start) | collective-permute-done | bytes 409632 | tf_op jit(solution)/shard_map/ppermute | solution.py:274
  10.8 13.9 %all_to_all.15.got = f32[4,256,128]{2,1,0:T(8,128)S(1)} all-to-all(f32[4,256,128]{2,1,0:T(8,128)S(1)} %pair_terms.1), channel_id=1, replica_groups=mesh['z_hi'=2,'y'=4,'z_lo'=8,'x'=4,'core'=2] {'x'}, dimensions={0} | all-to-all | bytes 1048576 | tf_op jit(solution)/shard_map/all_to_all | solution.py:277
  24.7 4.5 %all-to-all-start.2 = ((f32[4,2,8,512]{3,2,1,0:T(8,128)}), f32[4,2,8,512]{3,2,1,0:T(8,128)S(1)}, u32[]{:S(2)}, u32[]{:S(2)}) async-start(f32[4,2,8,512]{3,2,1,0:T(8,128)} %get-tuple-element.13), calls=%async_computation.2 | async-start | bytes 262144 | tf_op jit(solution)/shard_map/all_to_all | solution.py:276
  29.2 0.7 %split_terms.1 = (f32[8,24,128]{2,1,0:T(8,128)}, f32[3,32,128]{2,1,0:T(8,128)S(1)}) custom-call(f32[4,256,128]{2,1,0:T(8,128)S(1)} %all_to_all.15.got), custom_call_target="tpu_custom_call" | custom-call | flops 100000 | bytes 700000 | tf_op jit(solution)/shard_map/split_terms/pallas_call | solution.py:182
  29.8 5.3 %all-to-all-done.2 = f32[4,2,8,512]{3,2,1,0:T(8,128)S(1)} async-done(((f32[4,2,8,512]{3,2,1,0:T(8,128)}), f32[4,2,8,512]{3,2,1,0:T(8,128)S(1)}, u32[]{:S(2)}, u32[]{:S(2)}) %all-to-all-start.2) | async-done | bytes 131104 | tf_op jit(solution)/shard_map/all_to_all | solution.py:276
  35.1 12.6 %all-to-all-start.1 = ((f32[8,24,128]{2,1,0:T(8,128)}), f32[8,24,128]{2,1,0:T(8,128)S(1)}, u32[]{:S(2)}, u32[]{:S(2)}) async-start(f32[8,24,128]{2,1,0:T(8,128)} %get-tuple-element.11), calls=%async_computation.1 | async-start | bytes 196608 | tf_op jit(solution)/shard_map/all_to_all | solution.py:286
  47.8 8.2 %collective-permute-start.2 = (f32[8,512]{1,0:T(8,128)S(1)}, f32[8,512]{1,0:T(8,128)S(1)}, u32[]{:S(2)}, u32[]{:S(2)}) collective-permute-start(f32[8,512]{1,0:T(8,128)S(1)} %get-tuple-element.17), channel_id=1, source_target_pairs={{0,256},{256,0},{1,257},{257,1},{2,258},{258,2},{3,259},{259,3},{4... | collective-permute-start | bytes 49160 | tf_op jit(solution)/shard_map/ppermute | solution.py:279
  56.0 3.4 %collective-permute-start.1 = (f32[3,32,128]{2,1,0:T(8,128)S(1)}, f32[3,32,128]{2,1,0:T(8,128)S(1)}, u32[]{:S(2)}, u32[]{:S(2)}) collective-permute-start(f32[3,32,128]{2,1,0:T(8,128)S(1)} %get-tuple-element.12), channel_id=1, source_target_pairs={{0,8},{1,9},{2,10},{3,11},{8,16},{9,17},{10,18},{11,19},{16,24},{1... | collective-permute-start | bytes 147464 | tf_op jit(solution)/shard_map/ppermute | solution.py:285
  59.4 0.9 %constant_dynamic-slice_fusion = f32[48,64]{0,1:T(8,128)S(1)} fusion(f32[3072,64]{0,1:T(8,128)} %param.10, s32[]{:T(128)S(6)} %select_n.3), kind=kLoop, calls=%fused_computation.7 | loop fusion | bytes 24580 | tf_op jit(solution)/shard_map/dynamic_slice | solution.py:275
  60.3 0.1 copy.13
  60.4 1.8 %collective-permute-done.2.away = f32[8,512]{1,0:T(8,128)S(1)} collective-permute-done((f32[8,512]{1,0:T(8,128)S(1)}, f32[8,512]{1,0:T(8,128)S(1)}, u32[]{:S(2)}, u32[]{:S(2)}) %collective-permute-start.2) | collective-permute-done | bytes 16416 | tf_op jit(solution)/shard_map/ppermute | solution.py:279
  62.2 0.0 collective-permute-done.1.beside
  62.2 0.0 copy-done
  62.2 0.0 copy-done.1
  62.2 1.6 %ar_terms.1 = f32[8,512]{1,0:T(8,128)} custom-call(s32[10]{0:T(128)S(1)} %copy-done.1, f32[10,64]{1,0:T(8,128)S(1)} %copy-done, f32[8,32,128]{2,1,0:T(8,128)S(1)} %bitcast.7, f32[3,32,128]{2,1,0:T(8,128)S(1)} %collective-permute-done.1.beside, f32[8,512]{1,0:T(8,128)S(1)} %get-tuple-element.18.home, f32[8,512]{1,0:T(8,128)S(1)} %collective-permute-done.2.away), custom_call_target="tpu_custom_call" | custom-call | flops 2000000 | bytes 400000 | tf_op jit(solution)/shard_map/ar_terms/pallas_call | solution.py:251
  63.9 0.0 all-to-all-done.1
  63.9 0.1 fusion.2
  64.0 0.0 copy-done.2
  64.0 0.0 copy-done.3
  64.0 0.6 divide_subtract_fusion
  (5 shorter events, 0.1 us)
Async XLA Ops:
  7.0 55.3 %copy-start = (f32[10,64]{1,0:T(8,128)S(1)}, f32[10,64]{1,0:T(8,128)}, u32[]{:S(2)}) copy-start(f32[10,64]{1,0:T(8,128)} %weights.1) | copy-start | bytes 7684
  7.0 55.3 %copy-start.1 = (s32[10]{0:T(128)S(1)}, s32[10]{0:T(128)}, u32[]{:S(2)}) copy-start(s32[10]{0:T(128)} %lags.1) | copy-start | bytes 124
  7.0 57.0 %copy-start.2 = (f32[48,64]{1,0:T(8,128)S(1)}, f32[48,64]{1,0:T(8,128)}, u32[]{:S(2)}) copy-start(f32[48,64]{1,0:T(8,128)} %param.14) | copy-start | bytes 36868
  7.0 57.0 %copy-start.3 = (f32[48,64]{1,0:T(8,128)S(1)}, f32[48,64]{1,0:T(8,128)}, u32[]{:S(2)}) copy-start(f32[48,64]{1,0:T(8,128)} %param.15) | copy-start | bytes 36868
  7.0 3.8 %collective-permute-start = (f32[800,128]{1,0:T(8,128)S(1)}, f32[800,128]{1,0:T(8,128)S(1)}, u32[]{:S(2)}, u32[]{:S(2)}) collective-permute-start(f32[800,128]{1,0:T(8,128)S(1)} %get-tuple-element.10), channel_id=1, source_target_pairs={{0,1},{1,0},{2,3},{3,2},{4,5},{5,4},{6,7},{7,6},{8,9},{9,8},{10,11... | collective-permute-start | bytes 1228808 | tf_op jit(solution)/shard_map/ppermute | solution.py:274
  24.7 10.4 %all-to-all-start.2 = ((f32[4,2,8,512]{3,2,1,0:T(8,128)}), f32[4,2,8,512]{3,2,1,0:T(8,128)S(1)}, u32[]{:S(2)}, u32[]{:S(2)}) async-start(f32[4,2,8,512]{3,2,1,0:T(8,128)} %get-tuple-element.13), calls=%async_computation.2 | async-start | bytes 262144 | tf_op jit(solution)/shard_map/all_to_all | solution.py:276
  35.1 28.7 %all-to-all-start.1 = ((f32[8,24,128]{2,1,0:T(8,128)}), f32[8,24,128]{2,1,0:T(8,128)S(1)}, u32[]{:S(2)}, u32[]{:S(2)}) async-start(f32[8,24,128]{2,1,0:T(8,128)} %get-tuple-element.11), calls=%async_computation.1 | async-start | bytes 196608 | tf_op jit(solution)/shard_map/all_to_all | solution.py:286
  47.8 14.4 %collective-permute-start.2 = (f32[8,512]{1,0:T(8,128)S(1)}, f32[8,512]{1,0:T(8,128)S(1)}, u32[]{:S(2)}, u32[]{:S(2)}) collective-permute-start(f32[8,512]{1,0:T(8,128)S(1)} %get-tuple-element.17), channel_id=1, source_target_pairs={{0,256},{256,0},{1,257},{257,1},{2,258},{258,2},{3,259},{259,3},{4... | collective-permute-start | bytes 49160 | tf_op jit(solution)/shard_map/ppermute | solution.py:279
  56.0 6.2 %collective-permute-start.1 = (f32[3,32,128]{2,1,0:T(8,128)S(1)}, f32[3,32,128]{2,1,0:T(8,128)S(1)}, u32[]{:S(2)}, u32[]{:S(2)}) collective-permute-start(f32[3,32,128]{2,1,0:T(8,128)S(1)} %get-tuple-element.12), channel_id=1, source_target_pairs={{0,8},{1,9},{2,10},{3,11},{8,16},{9,17},{10,18},{11,19},{16,24},{1... | collective-permute-start | bytes 147464 | tf_op jit(solution)/shard_map/ppermute | solution.py:285

commit v4 on v3

--- a/solution.py
+++ b/solution.py
@@ -24,7 +24,6 @@
 FEEDER_AXES, TM_AXES = AXES[:2], AXES[2:]
 PLANES, PLANE = 8, 8
 TM = PLANES * PLANE
-FEEDER = 8
 SHARE = 48
 BAND = 8
 SPAN = 512
@@ -36,6 +35,10 @@
 CHUNKS = (HOPS + 1) * TILES
 
 
+def gray(place):
+    return place ^ (place >> 1)
+
+
 def place_of(axes):
     place = 0
     for axis in axes:
@@ -43,7 +46,9 @@
     return place
 
 
-def main_kernel(observed, words, factor, time, keep, send, time_out, total, *, steps, planes):
+def main_kernel(
+    observed, words, factor, time, keep, send, time_keep, time_send, total, *, steps, planes
+):
     step = pl.program_id(0)
     factor_half = factor[...].astype(jnp.bfloat16)
     time_half = time[...].astype(jnp.bfloat16)
@@ -101,10 +106,16 @@
 
     @pl.when(step == steps - 1)
     def _():
-        z_hi = lax.axis_index("z_hi")
-        for band in range(FEEDER):
-            z, y = band >> 2, band & 3
-            time_out[y, z_hi ^ z] = DATA_WEIGHT * total[BAND * band : BAND * band + BAND]
+        z_hi, y_ring = lax.axis_index("z_hi"), gray(lax.axis_index("y"))
+        for near in range(4):
+            far = near ^ y_ring
+            for z in range(2):
+                band = (z ^ z_hi) * 4 + (far ^ (far >> 1))
+                rows_out = DATA_WEIGHT * total[pl.ds(pl.multiple_of(band * BAND, BAND), BAND), :]
+                if near & 1:
+                    time_send[near >> 1, z] = rows_out
+                else:
+                    time_keep[near >> 1, z] = rows_out
 
 
 def main_terms(observed, words, factor, time, steps=4):
@@ -123,13 +134,15 @@
         out_specs=[
             pl.BlockSpec((half_rows, 128), lambda s: (0, 0)),
             pl.BlockSpec((half_rows, 128), lambda s: (0, 0)),
-            pl.BlockSpec((4, 2, BAND, span), lambda s: (0, 0, 0, 0)),
+            pl.BlockSpec((2, 2, BAND, span), lambda s: (0, 0, 0, 0)),
+            pl.BlockSpec((2, 2, BAND, span), lambda s: (0, 0, 0, 0)),
         ],
         scratch_shapes=[pltpu.VMEM((ranks, span), jnp.float32)],
         out_shape=[
             jax.ShapeDtypeStruct((half_rows, 128), jnp.float32),
             jax.ShapeDtypeStruct((half_rows, 128), jnp.float32),
-            jax.ShapeDtypeStruct((4, 2, BAND, span), jnp.float32),
+            jax.ShapeDtypeStruct((2, 2, BAND, span), jnp.float32),
+            jax.ShapeDtypeStruct((2, 2, BAND, span), jnp.float32),
         ],
         cost_estimate=pl.CostEstimate(flops=805306368, bytes_accessed=6_000_000, transcendentals=0),
         compiler_params=pltpu.CompilerParams(vmem_limit_bytes=24 << 20),
@@ -270,12 +283,13 @@
     ranks = time_factor.shape[0]
     tm_place = lax.axis_index(TM_AXES)
 
-    keep, send, time_part = main_terms(observed, mask_words.T, feeder_factor.T, time_factor)
+    keep, send, bands, sent_bands = main_terms(observed, mask_words.T, feeder_factor.T, time_factor)
     got = lax.ppermute(send, "core", [(0, 1), (1, 0)])
     own_factor = lax.dynamic_slice_in_dim(feeder_factor, tm_place * SHARE, SHARE, 0)
-    bands = lax.all_to_all(time_part, "y", 0, 0, tiled=True)
-    got = lax.all_to_all(pair_terms(keep, got), "x", 0, 0, tiled=True)
-    bands = bands.sum(0)
+    bands = bands + lax.ppermute(sent_bands, "y", [(0, 1), (1, 0), (2, 3), (3, 2)])
+    pair = pair_terms(keep, got)
+    bands = bands[0] + lax.ppermute(bands[1], "y", [(0, 3), (3, 0), (1, 2), (2, 1)])
+    got = lax.all_to_all(pair, "x", 0, 0, tiled=True)
     away = lax.ppermute(bands[1], "z_hi", [(0, 1), (1, 0)])
 
     planes, passed = split_terms(got)

time: 65.2 us -> 57.9 us (0.89)
  the two profiles are of different devices: /device:TPU:32 before, /device:TPU:100 now
where the time goes in v4:
time: 57.9 us; the launch traced here: 57.3 us
  starting transfers between devices  37.7 us (65%)
  Pallas kernels  8.86 us (15%)
  waiting for transfers between devices  8.25 us (14%)
  local copies, waits for them, and re-layouts  1.12 us (2%)
  between operations  0.77 us (1%)
  other arithmetic  0.67 us (1%)
    all_to_all x1, starting transfers between devices, per_device(): share = lax.all_to_all(planes, 'z_lo', 0, 0, tiled=True)  11.7 us
    ppermute x1, starting transfers between devices, per_device(): away = lax.ppermute(bands[1], 'z_hi', [(0, 1), (1, 0)])  8.22 us
    pallas_call x1, Pallas kernels, main_terms(): pl.pallas_call(functools.partial(main_kernel, steps=steps, planes=PLANES...  5.74 us
    ppermute x1, starting transfers between devices, per_device(): lax.ppermute(bands[1], 'y', [(0, 3), (3, 0), (1, 2), (2, 1)])  4.92 us
    all_to_all x1, starting transfers between devices, per_device(): got = lax.all_to_all(pair, 'x', 0, 0, tiled=True)  4.8 us
    ppermute x1, starting transfers between devices, per_device(): lax.ppermute(sent_bands, 'y', [(0, 1), (1, 0), (2, 3), (3, 2)])  3.47 us
    ppermute x1, waiting for transfers between devices, per_device(): away = lax.ppermute(bands[1], 'z_hi', [(0, 1), (1, 0)])  2.73 us
    ppermute x1, waiting for transfers between devices, per_device(): lax.ppermute(sent_bands, 'y', [(0, 1), (1, 0), (2, 3), (3, 2)])  2.67 us
  transfers between devices with their start and end apart: 7, of which 4 were waited for; matrix products, arithmetic and copies ran while one was open for 2% of the time, Pallas kernels for 4%

profile of v4, /device:TPU:100, one launch (start us, length us, event | category | flops | bytes accessed | tf_op | source)
XLA Modules:
  0.0 57.3 jit_solution(8836068500435745453)
XLA Ops:
  0.6 5.7 %main_terms.1 = (f32[800,128]{1,0:T(8,128)S(1)}, f32[800,128]{1,0:T(8,128)S(1)}, f32[2,2,8,512]{3,2,1,0:T(8,128)S(1)}, f32[2,2,8,512]{3,2,1,0:T(8,128)S(1)}) custom-call(bf16[3072,512]{1,0:T(8,128)(2,1)} %observed.1, s32[64,3072]{1,0:T(8,128)} %bitcast.15, f32[64,3072]{1,0:T(8,128)} %bitcast.14, f32[64,512]{1,0:T(8,128)} %time.1), custom_call_target="tpu_custom_call" | custom-call | flops 805306368 | bytes 6000000 | tf_op jit(solution)/shard_map/main_terms/pallas_call | solution.py:125
  6.4 0.0 copy-start
  6.4 0.0 copy-start.1
  6.4 0.0 copy-start.2
  6.4 0.0 copy-start.3
  6.4 2.1 %collective-permute-start = (f32[800,128]{1,0:T(8,128)S(1)}, f32[800,128]{1,0:T(8,128)S(1)}, u32[]{:S(2)}, u32[]{:S(2)}) collective-permute-start(f32[800,128]{1,0:T(8,128)S(1)} %get-tuple-element.11), channel_id=1, source_target_pairs={{0,1},{1,0},{2,3},{3,2},{4,5},{5,4},{6,7},{7,6},{8,9},{9,8},{10,11... | collective-permute-start | bytes 1228808 | tf_op jit(solution)/shard_map/ppermute | solution.py:287
  8.5 1.7 %collective-permute-done.got = f32[800,128]{1,0:T(8,128)S(1)} collective-permute-done((f32[800,128]{1,0:T(8,128)S(1)}, f32[800,128]{1,0:T(8,128)S(1)}, u32[]{:S(2)}, u32[]{:S(2)}) %collective-permute-start) | collective-permute-done | bytes 409632 | tf_op jit(solution)/shard_map/ppermute | solution.py:287
  10.2 0.8 %pair_terms.1 = f32[4,256,128]{2,1,0:T(8,128)} custom-call(f32[800,128]{1,0:T(8,128)S(1)} %get-tuple-element.10.keep, f32[800,128]{1,0:T(8,128)S(1)} %collective-permute-done.got), custom_call_target="tpu_custom_call" | custom-call | flops 100000 | bytes 1400000 | tf_op jit(solution)/shard_map/pair_terms/pallas_call | solution.py:166
  11.0 4.8 %all-to-all-start = ((f32[4,256,128]{2,1,0:T(8,128)}), f32[4,256,128]{2,1,0:T(8,128)S(1)}, u32[]{:S(2)}, u32[]{:S(2)}) async-start(f32[4,256,128]{2,1,0:T(8,128)} %pair_terms.1), calls=%async_computation | async-start | bytes 1048576 | tf_op jit(solution)/shard_map/all_to_all | solution.py:292
  15.8 3.5 %collective-permute-start.2 = (f32[2,2,8,512]{3,2,1,0:T(8,128)S(1)}, f32[2,2,8,512]{3,2,1,0:T(8,128)S(1)}, u32[]{:S(2)}, u32[]{:S(2)}) collective-permute-start(f32[2,2,8,512]{3,2,1,0:T(8,128)S(1)} %get-tuple-element.15), channel_id=1, source_target_pairs={{0,64},{64,0},{128,192},{192,128},{1,65},{65,1},{129,193},{193,129... | collective-permute-start | bytes 196616 | tf_op jit(solution)/shard_map/ppermute | solution.py:289
  19.3 2.7 %collective-permute-done.2 = f32[2,2,8,512]{3,2,1,0:T(8,128)S(1)} collective-permute-done((f32[2,2,8,512]{3,2,1,0:T(8,128)S(1)}, f32[2,2,8,512]{3,2,1,0:T(8,128)S(1)}, u32[]{:S(2)}, u32[]{:S(2)}) %collective-permute-start.2) | collective-permute-done | bytes 65568 | tf_op jit(solution)/shard_map/ppermute | solution.py:289
  22.0 4.9 %collective-permute-start.3 = (f32[2,8,512]{2,1,0:T(8,128)S(1)}, f32[2,8,512]{2,1,0:T(8,128)S(1)}, u32[]{:S(2)}, u32[]{:S(2)}) collective-permute-start(f32[2,8,512]{2,1,0:T(8,128)S(1)} %slice_bitcast_fusion), channel_id=1, source_target_pairs={{0,192},{192,0},{64,128},{128,64},{1,193},{193,1},{65,129},{129,65... | collective-permute-start | bytes 98312 | tf_op jit(solution)/shard_map/ppermute | solution.py:291
  26.9 0.0 all-to-all-done.got
  27.0 0.7 %split_terms.1 = (f32[8,24,128]{2,1,0:T(8,128)}, f32[3,32,128]{2,1,0:T(8,128)S(1)}) custom-call(f32[4,256,128]{2,1,0:T(8,128)S(1)} %all-to-all-done.got), custom_call_target="tpu_custom_call" | custom-call | flops 100000 | bytes 700000 | tf_op jit(solution)/shard_map/split_terms/pallas_call | solution.py:195
  27.6 11.7 %all-to-all-start.1 = ((f32[8,24,128]{2,1,0:T(8,128)}), f32[8,24,128]{2,1,0:T(8,128)S(1)}, u32[]{:S(2)}, u32[]{:S(2)}) async-start(f32[8,24,128]{2,1,0:T(8,128)} %get-tuple-element.12), calls=%async_computation.1 | async-start | bytes 196608 | tf_op jit(solution)/shard_map/all_to_all | solution.py:300
  39.3 0.0 collective-permute-done.3
  39.4 8.2 %collective-permute-start.4 = (f32[8,512]{1,0:T(8,128)S(1)}, f32[8,512]{1,0:T(8,128)S(1)}, u32[]{:S(2)}, u32[]{:S(2)}) collective-permute-start(f32[8,512]{1,0:T(8,128)S(1)} %get-tuple-element.19), channel_id=1, source_target_pairs={{0,256},{256,0},{1,257},{257,1},{2,258},{258,2},{3,259},{259,3},{4... | collective-permute-start | bytes 49160 | tf_op jit(solution)/shard_map/ppermute | solution.py:293
  47.6 2.5 %collective-permute-start.1 = (f32[3,32,128]{2,1,0:T(8,128)S(1)}, f32[3,32,128]{2,1,0:T(8,128)S(1)}, u32[]{:S(2)}, u32[]{:S(2)}) collective-permute-start(f32[3,32,128]{2,1,0:T(8,128)S(1)} %get-tuple-element.13), channel_id=1, source_target_pairs={{0,8},{1,9},{2,10},{3,11},{8,16},{9,17},{10,18},{11,19},{16,24},{1... | collective-permute-start | bytes 147464 | tf_op jit(solution)/shard_map/ppermute | solution.py:299
  50.1 0.9 %constant_dynamic-slice_fusion = f32[48,64]{0,1:T(8,128)S(1)} fusion(f32[3072,64]{0,1:T(8,128)} %param.10, s32[]{:T(128)S(6)} %select_n.3), kind=kLoop, calls=%fused_computation.10 | loop fusion | bytes 24580 | tf_op jit(solution)/shard_map/dynamic_slice | solution.py:288
  51.0 0.1 copy.13
  51.1 2.7 %collective-permute-done.4.away = f32[8,512]{1,0:T(8,128)S(1)} collective-permute-done((f32[8,512]{1,0:T(8,128)S(1)}, f32[8,512]{1,0:T(8,128)S(1)}, u32[]{:S(2)}, u32[]{:S(2)}) %collective-permute-start.4) | collective-permute-done | bytes 16416 | tf_op jit(solution)/shard_map/ppermute | solution.py:293
  53.8 1.1 %collective-permute-done.1.beside = f32[3,32,128]{2,1,0:T(8,128)S(1)} collective-permute-done((f32[3,32,128]{2,1,0:T(8,128)S(1)}, f32[3,32,128]{2,1,0:T(8,128)S(1)}, u32[]{:S(2)}, u32[]{:S(2)}) %collective-permute-start.1) | collective-permute-done | bytes 49184 | tf_op jit(solution)/shard_map/ppermute | solution.py:299
  55.0 0.0 copy-done
  55.0 0.0 copy-done.1
  55.0 1.6 %ar_terms.1 = f32[8,512]{1,0:T(8,128)} custom-call(s32[10]{0:T(128)S(1)} %copy-done.1, f32[10,64]{1,0:T(8,128)S(1)} %copy-done, f32[8,32,128]{2,1,0:T(8,128)S(1)} %bitcast.13, f32[3,32,128]{2,1,0:T(8,128)S(1)} %collective-permute-done.1.beside, f32[8,512]{1,0:T(8,128)S(1)} %get-tuple-element.20.home, f32[8,512]{1,0:T(8,128)S(1)} %collective-permute-done.4.away), custom_call_target="tpu_custom_call" | custom-call | flops 2000000 | bytes 400000 | tf_op jit(solution)/shard_map/ar_terms/pallas_call | solution.py:264
  56.6 0.0 all-to-all-done.1
  56.6 0.1 fusion.3
  56.7 0.0 copy-done.2
  56.7 0.0 copy-done.3
  56.7 0.6 %divide_subtract_fusion = (f32[48,64]{1,0:T(8,128)}, f32[48,64]{1,0:T(8,128)}, f32[48,64]{1,0:T(8,128)}) fusion(f32[48,64]{1,0:T(8,128)S(1)} %copy.13, f32[24,64]{1,0:T(8,128)S(1)} %get-tuple-element.22, f32[24,64]{1,0:T(8,128)S(1)} %get-tuple-element.21, f32[48,64]{1,0:T(8,128)S(1)} %copy-done.2, f32[48,64]{1,0:T(8,128)S(1)} %copy-done.3), kind=kLoop, calls=%fused_computation.6 | loop fusion | flops 46080 | bytes 86016 | tf_op jit(solution)/shard_map/sub | solution.py:311
  (6 shorter events, 0.1 us)
Async XLA Ops:
  6.4 48.6 %copy-start = (f32[10,64]{1,0:T(8,128)S(1)}, f32[10,64]{1,0:T(8,128)}, u32[]{:S(2)}) copy-start(f32[10,64]{1,0:T(8,128)} %weights.1) | copy-start | bytes 7684
  6.4 48.6 %copy-start.1 = (s32[10]{0:T(128)S(1)}, s32[10]{0:T(128)}, u32[]{:S(2)}) copy-start(s32[10]{0:T(128)} %lags.1) | copy-start | bytes 124
  6.4 50.3 %copy-start.2 = (f32[48,64]{1,0:T(8,128)S(1)}, f32[48,64]{1,0:T(8,128)}, u32[]{:S(2)}) copy-start(f32[48,64]{1,0:T(8,128)} %param.14) | copy-start | bytes 36868
  6.4 50.3 %copy-start.3 = (f32[48,64]{1,0:T(8,128)S(1)}, f32[48,64]{1,0:T(8,128)}, u32[]{:S(2)}) copy-start(f32[48,64]{1,0:T(8,128)} %param.15) | copy-start | bytes 36868
  6.4 3.8 %collective-permute-start = (f32[800,128]{1,0:T(8,128)S(1)}, f32[800,128]{1,0:T(8,128)S(1)}, u32[]{:S(2)}, u32[]{:S(2)}) collective-permute-start(f32[800,128]{1,0:T(8,128)S(1)} %get-tuple-element.11), channel_id=1, source_target_pairs={{0,1},{1,0},{2,3},{3,2},{4,5},{5,4},{6,7},{7,6},{8,9},{9,8},{10,11... | collective-permute-start | bytes 1228808 | tf_op jit(solution)/shard_map/ppermute | solution.py:287
  11.0 15.9 %all-to-all-start = ((f32[4,256,128]{2,1,0:T(8,128)}), f32[4,256,128]{2,1,0:T(8,128)S(1)}, u32[]{:S(2)}, u32[]{:S(2)}) async-start(f32[4,256,128]{2,1,0:T(8,128)} %pair_terms.1), calls=%async_computation | async-start | bytes 1048576 | tf_op jit(solution)/shard_map/all_to_all | solution.py:292
  15.8 6.1 %collective-permute-start.2 = (f32[2,2,8,512]{3,2,1,0:T(8,128)S(1)}, f32[2,2,8,512]{3,2,1,0:T(8,128)S(1)}, u32[]{:S(2)}, u32[]{:S(2)}) collective-permute-start(f32[2,2,8,512]{3,2,1,0:T(8,128)S(1)} %get-tuple-element.15), channel_id=1, source_target_pairs={{0,64},{64,0},{128,192},{192,128},{1,65},{65,1},{129,193},{193,129... | collective-permute-start | bytes 196616 | tf_op jit(solution)/shard_map/ppermute | solution.py:289
  22.0 17.3 %collective-permute-start.3 = (f32[2,8,512]{2,1,0:T(8,128)S(1)}, f32[2,8,512]{2,1,0:T(8,128)S(1)}, u32[]{:S(2)}, u32[]{:S(2)}) collective-permute-start(f32[2,8,512]{2,1,0:T(8,128)S(1)} %slice_bitcast_fusion), channel_id=1, source_target_pairs={{0,192},{192,0},{64,128},{128,64},{1,193},{193,1},{65,129},{129,65... | collective-permute-start | bytes 98312 | tf_op jit(solution)/shard_map/ppermute | solution.py:291
  27.6 29.0 %all-to-all-start.1 = ((f32[8,24,128]{2,1,0:T(8,128)}), f32[8,24,128]{2,1,0:T(8,128)S(1)}, u32[]{:S(2)}, u32[]{:S(2)}) async-start(f32[8,24,128]{2,1,0:T(8,128)} %get-tuple-element.12), calls=%async_computation.1 | async-start | bytes 196608 | tf_op jit(solution)/shard_map/all_to_all | solution.py:300
  39.4 14.5 %collective-permute-start.4 = (f32[8,512]{1,0:T(8,128)S(1)}, f32[8,512]{1,0:T(8,128)S(1)}, u32[]{:S(2)}, u32[]{:S(2)}) collective-permute-start(f32[8,512]{1,0:T(8,128)S(1)} %get-tuple-element.19), channel_id=1, source_target_pairs={{0,256},{256,0},{1,257},{257,1},{2,258},{258,2},{3,259},{259,3},{4... | collective-permute-start | bytes 49160 | tf_op jit(solution)/shard_map/ppermute | solution.py:293
  47.6 7.4 %collective-permute-start.1 = (f32[3,32,128]{2,1,0:T(8,128)S(1)}, f32[3,32,128]{2,1,0:T(8,128)S(1)}, u32[]{:S(2)}, u32[]{:S(2)}) collective-permute-start(f32[3,32,128]{2,1,0:T(8,128)S(1)} %get-tuple-element.13), channel_id=1, source_target_pairs={{0,8},{1,9},{2,10},{3,11},{8,16},{9,17},{10,18},{11,19},{16,24},{1... | collective-permute-start | bytes 147464 | tf_op jit(solution)/shard_map/ppermute | solution.py:299

commit v5 on v4

--- a/solution.py
+++ b/solution.py
@@ -214,9 +214,7 @@
     return [jnp.where(inside, rolled[i], rolled[i + 1]) for i in range(count)]
 
 
-def ar_kernel(
-    lags, weights, plane, beside, home, away, time_grad, spans, errors, weight_rows
-):
+def ar_kernel(lags, weights, plane, beside, home, out, spans, errors, weight_rows):
     edge = HOPS * TILES
     for span in range(HOPS):
         for tile in range(TILES):
@@ -249,21 +247,20 @@
         carried = [part + gains[k] * tile for part, tile in zip(carried, moved)]
     for tile in range(TILES):
         at = slice(128 * tile, 128 * tile + 128)
-        time_grad[:, at] = (
+        out[:, at] = (
             home[:, at]
-            + away[:, at]
             + LAM_AR * (errors[tile] - carried[tile])
             + LAM_X * spans[own_tile + tile]
         )
 
 
-def ar_terms(lags, weights, plane, beside, home, away):
+def ar_terms(lags, weights, plane, beside, home):
     in_vmem = pl.BlockSpec(memory_space=pltpu.VMEM)
     in_smem = pl.BlockSpec(memory_space=pltpu.SMEM)
     tiles = (2 * HOPS + PLANE) * TILES
     return pl.pallas_call(
         ar_kernel,
-        in_specs=[in_smem] + [in_vmem] * 5,
+        in_specs=[in_smem] + [in_vmem] * 4,
         out_specs=in_vmem,
         out_shape=jax.ShapeDtypeStruct((BAND, SPAN), jnp.float32),
         scratch_shapes=[
@@ -274,7 +271,7 @@
         cost_estimate=pl.CostEstimate(flops=2_000_000, bytes_accessed=400_000, transcendentals=0),
         compiler_params=pltpu.CompilerParams(vmem_limit_bytes=8 << 20),
         name="ar_terms",
-    )(lags, weights, plane, beside, home, away)
+    )(lags, weights, plane, beside, home)
 
 
 def per_device(
@@ -299,7 +296,7 @@
     beside = lax.ppermute(passed, TM_AXES, pairs)
     share = lax.all_to_all(planes, "z_lo", 0, 0, tiled=True)
     share = share.sum(0)
-    time_grad = ar_terms(lags, ar_weight, plane, beside, bands[0], away)
+    time_grad = ar_terms(lags, ar_weight, plane, beside, bands[0]) + away
 
     grad_share = jnp.concatenate([share[:, :ranks], share[:, ranks:]], axis=0)
     factor_grad = grad_share + LAM_F * own_factor

time: 57.9 us -> 57.9 us (level)
  other arithmetic: 0.67 us -> 1.28 us
  Pallas kernels: 8.86 us -> 8.25 us
    ppermute x1, waiting for transfers between devices: 1.13 us -> 3.87 us  [per_device(): beside = lax.ppermute(passed, TM_AXES, pairs)]
    ppermute x1, waiting for transfers between devices: 2.73 us -> 0.01 us  [per_device(): away = lax.ppermute(bands[1], 'z_hi', [(0, 1), (1, 0)])]
    pallas_call x1, Pallas kernels: 1.62 us -> 1 us  [ar_terms(): pl.pallas_call(ar_kernel, in_specs=[in_smem] + [in_vmem] * 4, out_specs=i...]
    add x0 -> x1, other arithmetic: none -> 0.61 us  [per_device(): time_grad = ar_terms(lags, ar_weight, plane, beside, bands[0]) + away]
  transfers between devices with their start and end apart: 7 -> 7, of which waited for: 4 -> 3; matrix products, arithmetic and copies ran while one was open for 2% -> 3% of each run, Pallas kernels for 4% -> 3%
where the time goes in v5:
time: 57.9 us; the launch traced here: 57.3 us
  starting transfers between devices  37.7 us (65%)
  waiting for transfers between devices  8.26 us (14%)
  Pallas kernels  8.25 us (14%)
  other arithmetic  1.28 us (2%)
  local copies, waits for them, and re-layouts  1.12 us (2%)
  between operations  0.78 us (1%)
    all_to_all x1, starting transfers between devices, per_device(): share = lax.all_to_all(planes, 'z_lo', 0, 0, tiled=True)  11.7 us
    ppermute x1, starting transfers between devices, per_device(): away = lax.ppermute(bands[1], 'z_hi', [(0, 1), (1, 0)])  8.22 us
    pallas_call x1, Pallas kernels, main_terms(): pl.pallas_call(functools.partial(main_kernel, steps=steps, planes=PLANES...  5.74 us
    ppermute x1, starting transfers between devices, per_device(): lax.ppermute(bands[1], 'y', [(0, 3), (3, 0), (1, 2), (2, 1)])  4.92 us
    all_to_all x1, starting transfers between devices, per_device(): got = lax.all_to_all(pair, 'x', 0, 0, tiled=True)  4.8 us
    ppermute x1, waiting for transfers between devices, per_device(): beside = lax.ppermute(passed, TM_AXES, pairs)  3.87 us
    ppermute x1, starting transfers between devices, per_device(): lax.ppermute(sent_bands, 'y', [(0, 1), (1, 0), (2, 3), (3, 2)])  3.47 us
    ppermute x1, waiting for transfers between devices, per_device(): lax.ppermute(sent_bands, 'y', [(0, 1), (1, 0), (2, 3), (3, 2)])  2.67 us
  transfers between devices with their start and end apart: 7, of which 3 were waited for; matrix products, arithmetic and copies ran while one was open for 3% of the time, Pallas kernels for 3%

profile of v5, /device:TPU:100, one launch (start us, length us, event | category | flops | bytes accessed | tf_op | source)
XLA Modules:
  0.0 57.3 jit_solution(16795669526474688164)
XLA Ops:
  0.6 5.7 %main_terms.1 = (f32[800,128]{1,0:T(8,128)S(1)}, f32[800,128]{1,0:T(8,128)S(1)}, f32[2,2,8,512]{3,2,1,0:T(8,128)S(1)}, f32[2,2,8,512]{3,2,1,0:T(8,128)S(1)}) custom-call(bf16[3072,512]{1,0:T(8,128)(2,1)} %observed.1, s32[64,3072]{1,0:T(8,128)} %bitcast.15, f32[64,3072]{1,0:T(8,128)} %bitcast.14, f32[64,512]{1,0:T(8,128)} %time.1), custom_call_target="tpu_custom_call" | custom-call | flops 805306368 | bytes 6000000 | tf_op jit(solution)/shard_map/main_terms/pallas_call | solution.py:125
  6.4 0.0 copy-start
  6.4 0.0 copy-start.1
  6.4 0.0 copy-start.2
  6.4 0.0 copy-start.3
  6.4 2.1 %collective-permute-start = (f32[800,128]{1,0:T(8,128)S(1)}, f32[800,128]{1,0:T(8,128)S(1)}, u32[]{:S(2)}, u32[]{:S(2)}) collective-permute-start(f32[800,128]{1,0:T(8,128)S(1)} %get-tuple-element.11), channel_id=1, source_target_pairs={{0,1},{1,0},{2,3},{3,2},{4,5},{5,4},{6,7},{7,6},{8,9},{9,8},{10,11... | collective-permute-start | bytes 1228808 | tf_op jit(solution)/shard_map/ppermute | solution.py:284
  8.5 1.7 %collective-permute-done.got = f32[800,128]{1,0:T(8,128)S(1)} collective-permute-done((f32[800,128]{1,0:T(8,128)S(1)}, f32[800,128]{1,0:T(8,128)S(1)}, u32[]{:S(2)}, u32[]{:S(2)}) %collective-permute-start) | collective-permute-done | bytes 409632 | tf_op jit(solution)/shard_map/ppermute | solution.py:284
  10.2 0.8 %pair_terms.1 = f32[4,256,128]{2,1,0:T(8,128)} custom-call(f32[800,128]{1,0:T(8,128)S(1)} %get-tuple-element.10.keep, f32[800,128]{1,0:T(8,128)S(1)} %collective-permute-done.got), custom_call_target="tpu_custom_call" | custom-call | flops 100000 | bytes 1400000 | tf_op jit(solution)/shard_map/pair_terms/pallas_call | solution.py:166
  11.0 4.8 %all-to-all-start = ((f32[4,256,128]{2,1,0:T(8,128)}), f32[4,256,128]{2,1,0:T(8,128)S(1)}, u32[]{:S(2)}, u32[]{:S(2)}) async-start(f32[4,256,128]{2,1,0:T(8,128)} %pair_terms.1), calls=%async_computation | async-start | bytes 1048576 | tf_op jit(solution)/shard_map/all_to_all | solution.py:289
  15.8 3.5 %collective-permute-start.2 = (f32[2,2,8,512]{3,2,1,0:T(8,128)S(1)}, f32[2,2,8,512]{3,2,1,0:T(8,128)S(1)}, u32[]{:S(2)}, u32[]{:S(2)}) collective-permute-start(f32[2,2,8,512]{3,2,1,0:T(8,128)S(1)} %get-tuple-element.15), channel_id=1, source_target_pairs={{0,64},{64,0},{128,192},{192,128},{1,65},{65,1},{129,193},{193,129... | collective-permute-start | bytes 196616 | tf_op jit(solution)/shard_map/ppermute | solution.py:286
  19.3 2.7 %collective-permute-done.2 = f32[2,2,8,512]{3,2,1,0:T(8,128)S(1)} collective-permute-done((f32[2,2,8,512]{3,2,1,0:T(8,128)S(1)}, f32[2,2,8,512]{3,2,1,0:T(8,128)S(1)}, u32[]{:S(2)}, u32[]{:S(2)}) %collective-permute-start.2) | collective-permute-done | bytes 65568 | tf_op jit(solution)/shard_map/ppermute | solution.py:286
  22.0 4.9 %collective-permute-start.3 = (f32[2,8,512]{2,1,0:T(8,128)S(1)}, f32[2,8,512]{2,1,0:T(8,128)S(1)}, u32[]{:S(2)}, u32[]{:S(2)}) collective-permute-start(f32[2,8,512]{2,1,0:T(8,128)S(1)} %slice_bitcast_fusion), channel_id=1, source_target_pairs={{0,192},{192,0},{64,128},{128,64},{1,193},{193,1},{65,129},{129,65... | collective-permute-start | bytes 98312 | tf_op jit(solution)/shard_map/ppermute | solution.py:288
  26.9 0.0 all-to-all-done.got
  27.0 0.7 %split_terms.1 = (f32[8,24,128]{2,1,0:T(8,128)}, f32[3,32,128]{2,1,0:T(8,128)S(1)}) custom-call(f32[4,256,128]{2,1,0:T(8,128)S(1)} %all-to-all-done.got), custom_call_target="tpu_custom_call" | custom-call | flops 100000 | bytes 700000 | tf_op jit(solution)/shard_map/split_terms/pallas_call | solution.py:195
  27.6 11.7 %all-to-all-start.1 = ((f32[8,24,128]{2,1,0:T(8,128)}), f32[8,24,128]{2,1,0:T(8,128)S(1)}, u32[]{:S(2)}, u32[]{:S(2)}) async-start(f32[8,24,128]{2,1,0:T(8,128)} %get-tuple-element.12), calls=%async_computation.1 | async-start | bytes 196608 | tf_op jit(solution)/shard_map/all_to_all | solution.py:297
  39.3 0.0 collective-permute-done.3
  39.4 8.2 %collective-permute-start.4 = (f32[8,512]{1,0:T(8,128)S(1)}, f32[8,512]{1,0:T(8,128)S(1)}, u32[]{:S(2)}, u32[]{:S(2)}) collective-permute-start(f32[8,512]{1,0:T(8,128)S(1)} %get-tuple-element.19), channel_id=1, source_target_pairs={{0,256},{256,0},{1,257},{257,1},{2,258},{258,2},{3,259},{259,3},{4... | collective-permute-start | bytes 49160 | tf_op jit(solution)/shard_map/ppermute | solution.py:290
  47.6 2.5 %collective-permute-start.1 = (f32[3,32,128]{2,1,0:T(8,128)S(1)}, f32[3,32,128]{2,1,0:T(8,128)S(1)}, u32[]{:S(2)}, u32[]{:S(2)}) collective-permute-start(f32[3,32,128]{2,1,0:T(8,128)S(1)} %get-tuple-element.13), channel_id=1, source_target_pairs={{0,8},{1,9},{2,10},{3,11},{8,16},{9,17},{10,18},{11,19},{16,24},{1... | collective-permute-start | bytes 147464 | tf_op jit(solution)/shard_map/ppermute | solution.py:296
  50.1 0.9 %constant_dynamic-slice_fusion = f32[48,64]{0,1:T(8,128)S(1)} fusion(f32[3072,64]{0,1:T(8,128)} %param.10, s32[]{:T(128)S(6)} %select_n.3), kind=kLoop, calls=%fused_computation.10 | loop fusion | bytes 24580 | tf_op jit(solution)/shard_map/dynamic_slice | solution.py:285
  51.0 0.1 copy.13
  51.1 3.9 %collective-permute-done.1.beside = f32[3,32,128]{2,1,0:T(8,128)S(1)} collective-permute-done((f32[3,32,128]{2,1,0:T(8,128)S(1)}, f32[3,32,128]{2,1,0:T(8,128)S(1)}, u32[]{:S(2)}, u32[]{:S(2)}) %collective-permute-start.1) | collective-permute-done | bytes 49184 | tf_op jit(solution)/shard_map/ppermute | solution.py:296
  55.0 0.0 copy-done
  55.0 0.0 copy-done.1
  55.0 1.0 %ar_terms.1 = f32[8,512]{1,0:T(8,128)S(1)} custom-call(s32[10]{0:T(128)S(1)} %copy-done.1, f32[10,64]{1,0:T(8,128)S(1)} %copy-done, f32[8,32,128]{2,1,0:T(8,128)S(1)} %bitcast.13, f32[3,32,128]{2,1,0:T(8,128)S(1)} %collective-permute-done.1.beside, f32[8,512]{1,0:T(8,128)S(1)} %get-tuple-element.20.home), custom_call_target="tpu_custom_call" | custom-call | flops 2000000 | bytes 400000 | tf_op jit(solution)/shard_map/ar_terms/pallas_call | solution.py:261
  56.0 0.0 collective-permute-done.4
  56.0 0.6 %add.43 = f32[8,512]{1,0:T(8,128)} add(f32[8,512]{1,0:T(8,128)S(1)} %ar_terms.1, f32[8,512]{1,0:T(8,128)S(1)} %collective-permute-done.4) | non-fusion elementwise | flops 4096 | bytes 49152 | tf_op jit(solution)/shard_map/add | solution.py:299
  56.6 0.0 all-to-all-done.1
  56.6 0.1 fusion.3
  56.7 0.0 copy-done.2
  56.7 0.0 copy-done.3
  56.7 0.6 %divide_subtract_fusion = (f32[48,64]{1,0:T(8,128)}, f32[48,64]{1,0:T(8,128)}, f32[48,64]{1,0:T(8,128)}) fusion(f32[48,64]{1,0:T(8,128)S(1)} %copy.13, f32[24,64]{1,0:T(8,128)S(1)} %get-tuple-element.22, f32[24,64]{1,0:T(8,128)S(1)} %get-tuple-element.21, f32[48,64]{1,0:T(8,128)S(1)} %copy-done.2, f32[48,64]{1,0:T(8,128)S(1)} %copy-done.3), kind=kLoop, calls=%fused_computation.6 | loop fusion | flops 46080 | bytes 86016 | tf_op jit(solution)/shard_map/sub | solution.py:308
  (6 shorter events, 0.1 us)
Async XLA Ops:
  6.4 48.6 %copy-start = (f32[10,64]{1,0:T(8,128)S(1)}, f32[10,64]{1,0:T(8,128)}, u32[]{:S(2)}) copy-start(f32[10,64]{1,0:T(8,128)} %weights.1) | copy-start | bytes 7684
  6.4 48.6 %copy-start.1 = (s32[10]{0:T(128)S(1)}, s32[10]{0:T(128)}, u32[]{:S(2)}) copy-start(s32[10]{0:T(128)} %lags.1) | copy-start | bytes 124
  6.4 50.3 %copy-start.2 = (f32[48,64]{1,0:T(8,128)S(1)}, f32[48,64]{1,0:T(8,128)}, u32[]{:S(2)}) copy-start(f32[48,64]{1,0:T(8,128)} %param.14) | copy-start | bytes 36868
  6.4 50.3 %copy-start.3 = (f32[48,64]{1,0:T(8,128)S(1)}, f32[48,64]{1,0:T(8,128)}, u32[]{:S(2)}) copy-start(f32[48,64]{1,0:T(8,128)} %param.15) | copy-start | bytes 36868
  6.4 3.8 %collective-permute-start = (f32[800,128]{1,0:T(8,128)S(1)}, f32[800,128]{1,0:T(8,128)S(1)}, u32[]{:S(2)}, u32[]{:S(2)}) collective-permute-start(f32[800,128]{1,0:T(8,128)S(1)} %get-tuple-element.11), channel_id=1, source_target_pairs={{0,1},{1,0},{2,3},{3,2},{4,5},{5,4},{6,7},{7,6},{8,9},{9,8},{10,11... | collective-permute-start | bytes 1228808 | tf_op jit(solution)/shard_map/ppermute | solution.py:284
  11.0 15.9 %all-to-all-start = ((f32[4,256,128]{2,1,0:T(8,128)}), f32[4,256,128]{2,1,0:T(8,128)S(1)}, u32[]{:S(2)}, u32[]{:S(2)}) async-start(f32[4,256,128]{2,1,0:T(8,128)} %pair_terms.1), calls=%async_computation | async-start | bytes 1048576 | tf_op jit(solution)/shard_map/all_to_all | solution.py:289
  15.8 6.1 %collective-permute-start.2 = (f32[2,2,8,512]{3,2,1,0:T(8,128)S(1)}, f32[2,2,8,512]{3,2,1,0:T(8,128)S(1)}, u32[]{:S(2)}, u32[]{:S(2)}) collective-permute-start(f32[2,2,8,512]{3,2,1,0:T(8,128)S(1)} %get-tuple-element.15), channel_id=1, source_target_pairs={{0,64},{64,0},{128,192},{192,128},{1,65},{65,1},{129,193},{193,129... | collective-permute-start | bytes 196616 | tf_op jit(solution)/shard_map/ppermute | solution.py:286
  22.0 17.3 %collective-permute-start.3 = (f32[2,8,512]{2,1,0:T(8,128)S(1)}, f32[2,8,512]{2,1,0:T(8,128)S(1)}, u32[]{:S(2)}, u32[]{:S(2)}) collective-permute-start(f32[2,8,512]{2,1,0:T(8,128)S(1)} %slice_bitcast_fusion), channel_id=1, source_target_pairs={{0,192},{192,0},{64,128},{128,64},{1,193},{193,1},{65,129},{129,65... | collective-permute-start | bytes 98312 | tf_op jit(solution)/shard_map/ppermute | solution.py:288
  27.6 29.0 %all-to-all-start.1 = ((f32[8,24,128]{2,1,0:T(8,128)}), f32[8,24,128]{2,1,0:T(8,128)S(1)}, u32[]{:S(2)}, u32[]{:S(2)}) async-start(f32[8,24,128]{2,1,0:T(8,128)} %get-tuple-element.12), calls=%async_computation.1 | async-start | bytes 196608 | tf_op jit(solution)/shard_map/all_to_all | solution.py:297
  39.4 16.6 %collective-permute-start.4 = (f32[8,512]{1,0:T(8,128)S(1)}, f32[8,512]{1,0:T(8,128)S(1)}, u32[]{:S(2)}, u32[]{:S(2)}) collective-permute-start(f32[8,512]{1,0:T(8,128)S(1)} %get-tuple-element.19), channel_id=1, source_target_pairs={{0,256},{256,0},{1,257},{257,1},{2,258},{258,2},{3,259},{259,3},{4... | collective-permute-start | bytes 49160 | tf_op jit(solution)/shard_map/ppermute | solution.py:290
  47.6 7.4 %collective-permute-start.1 = (f32[3,32,128]{2,1,0:T(8,128)S(1)}, f32[3,32,128]{2,1,0:T(8,128)S(1)}, u32[]{:S(2)}, u32[]{:S(2)}) collective-permute-start(f32[3,32,128]{2,1,0:T(8,128)S(1)} %get-tuple-element.13), channel_id=1, source_target_pairs={{0,8},{1,9},{2,10},{3,11},{8,16},{9,17},{10,18},{11,19},{16,24},{1... | collective-permute-start | bytes 147464 | tf_op jit(solution)/shard_map/ppermute | solution.py:296

commit v6 on v5

--- a/solution.py
+++ b/solution.py
@@ -30,7 +30,6 @@
 TILES = SPAN // 128
 MAIN_ROWS = PLANES * SHARE // 2
 BAND_ROWS = BAND * TILES
-ROWS = MAIN_ROWS + 2 * BAND_ROWS
 HOPS = 3
 CHUNKS = (HOPS + 1) * TILES
 
@@ -47,7 +46,7 @@
 
 
 def main_kernel(
-    observed, words, factor, time, keep, send, time_keep, time_send, total, *, steps, planes
+    observed, words, factor, time, keep, send, own_band, time_keep, time_send, total, *, steps, planes
 ):
     step = pl.program_id(0)
     factor_half = factor[...].astype(jnp.bfloat16)
@@ -97,8 +96,8 @@
         own = time[pl.ds(pl.multiple_of(place_of(FEEDER_AXES) * BAND, BAND), BAND), :]
         for tile in range(TILES):
             at = PLANE // 2 * MAIN_ROWS + BAND * tile
-            keep[at : at + BAND] = own[:, 128 * tile : 128 * tile + 128]
             send[at : at + BAND] = own[:, 128 * tile : 128 * tile + 128]
+            own_band[BAND * tile : BAND * tile + BAND] = own[:, 128 * tile : 128 * tile + 128]
 
     @pl.when(step > 0)
     def _():
@@ -121,7 +120,7 @@
 def main_terms(observed, words, factor, time, steps=4):
     feeders, span = observed.shape
     ranks, block = factor.shape[0], feeders // steps
-    half_rows = PLANE // 2 * MAIN_ROWS + BAND_ROWS
+    half_rows = PLANE // 2 * MAIN_ROWS
     return pl.pallas_call(
         functools.partial(main_kernel, steps=steps, planes=PLANES // steps),
         grid=(steps,),
@@ -133,14 +132,16 @@
         ],
         out_specs=[
             pl.BlockSpec((half_rows, 128), lambda s: (0, 0)),
-            pl.BlockSpec((half_rows, 128), lambda s: (0, 0)),
+            pl.BlockSpec((half_rows + BAND_ROWS, 128), lambda s: (0, 0)),
+            pl.BlockSpec((BAND_ROWS, 128), lambda s: (0, 0)),
             pl.BlockSpec((2, 2, BAND, span), lambda s: (0, 0, 0, 0)),
             pl.BlockSpec((2, 2, BAND, span), lambda s: (0, 0, 0, 0)),
         ],
         scratch_shapes=[pltpu.VMEM((ranks, span), jnp.float32)],
         out_shape=[
             jax.ShapeDtypeStruct((half_rows, 128), jnp.float32),
-            jax.ShapeDtypeStruct((half_rows, 128), jnp.float32),
+            jax.ShapeDtypeStruct((half_rows + BAND_ROWS, 128), jnp.float32),
+            jax.ShapeDtypeStruct((BAND_ROWS, 128), jnp.float32),
             jax.ShapeDtypeStruct((2, 2, BAND, span), jnp.float32),
             jax.ShapeDtypeStruct((2, 2, BAND, span), jnp.float32),
         ],
@@ -150,60 +151,35 @@
     )(*(pltpu.with_memory_space_constraint(a, pltpu.HBM) for a in (observed, words, factor, time)))
 
 
-def pair_kernel(keep, got, out):
+def pair_kernel(keep, own_band, got, out, both):
     first = lax.axis_index("core") == 0
-    tail = PLANE // 2 * MAIN_ROWS
-    mine, other = keep[tail:], got[tail:]
+    mine, other = own_band[...], got[PLANE // 2 * MAIN_ROWS :]
+    both[0] = jnp.where(first, mine, other)
+    both[1] = jnp.where(first, other, mine)
     for x in range(PLANE // 2):
         at = slice(x * MAIN_ROWS, (x + 1) * MAIN_ROWS)
-        out[x, :MAIN_ROWS] = keep[at] + got[at]
-        out[x, MAIN_ROWS : MAIN_ROWS + BAND_ROWS] = jnp.where(first, mine, other)
-        out[x, MAIN_ROWS + BAND_ROWS :] = jnp.where(first, other, mine)
-
-
-def pair_terms(keep, got):
-    in_vmem = pl.BlockSpec(memory_space=pltpu.VMEM)
-    return pl.pallas_call(
-        pair_kernel,
-        in_specs=[in_vmem, in_vmem],
-        out_specs=in_vmem,
-        out_shape=jax.ShapeDtypeStruct((PLANE // 2, ROWS, 128), jnp.float32),
-        cost_estimate=pl.CostEstimate(flops=100_000, bytes_accessed=1_400_000, transcendentals=0),
-        compiler_params=pltpu.CompilerParams(vmem_limit_bytes=8 << 20),
-        name="pair_terms",
-    )(keep, got)
-
-
-def split_kernel(got, planes, passed):
-    total = got[0, :MAIN_ROWS]
+        out[x] = keep[at] + got[at]
+
+
+def sum_kernel(got, planes):
+    total = got[0]
     for x in range(1, PLANE // 2):
-        total = total + got[x, :MAIN_ROWS]
+        total = total + got[x]
     half = SHARE // 2
     for z in range(PLANES):
         planes[z] = total[half * z : half * z + half]
-    late = place_of(AXES[3:]) < PLANE // 2
-    for span in range(HOPS):
-        ends = []
-        for source in (PLANE - HOPS + span, span):
-            at = MAIN_ROWS + BAND_ROWS * (source & 1)
-            ends.append(got[source >> 1, at : at + BAND_ROWS])
-        passed[span] = jnp.where(late, ends[0], ends[1])
-
-
-def split_terms(got):
+
+
+def on_chip(kernel, args, outs):
     in_vmem = pl.BlockSpec(memory_space=pltpu.VMEM)
     return pl.pallas_call(
-        split_kernel,
-        in_specs=[in_vmem],
-        out_specs=[in_vmem, in_vmem],
-        out_shape=[
-            jax.ShapeDtypeStruct((PLANES, SHARE // 2, 128), jnp.float32),
-            jax.ShapeDtypeStruct((HOPS, BAND_ROWS, 128), jnp.float32),
-        ],
-        cost_estimate=pl.CostEstimate(flops=100_000, bytes_accessed=700_000, transcendentals=0),
+        kernel,
+        in_specs=[in_vmem] * len(args),
+        out_specs=[in_vmem] * len(outs),
+        out_shape=[jax.ShapeDtypeStruct(shape, jnp.float32) for shape in outs],
+        cost_estimate=pl.CostEstimate(flops=100_000, bytes_accessed=1_000_000, transcendentals=0),
         compiler_params=pltpu.CompilerParams(vmem_limit_bytes=8 << 20),
-        name="split_terms",
-    )(got)
+    )(*args)
 
 
 def shifted_tiles(start, count, read):
@@ -214,19 +190,17 @@
     return [jnp.where(inside, rolled[i], rolled[i + 1]) for i in range(count)]
 
 
-def ar_kernel(lags, weights, plane, beside, home, out, spans, errors, weight_rows):
-    edge = HOPS * TILES
-    for span in range(HOPS):
-        for tile in range(TILES):
-            value = beside[span, BAND * tile : BAND * tile + BAND]
-            spans[span * TILES + tile] = value
-            spans[edge + PLANE * TILES + span * TILES + tile] = value
-    for span in range(PLANE):
-        for tile in range(TILES):
-            spans[edge + span * TILES + tile] = plane[span, BAND * tile : BAND * tile + BAND]
+def ar_kernel(lags, weights, before, both, after, far, home, out, spans, errors, weight_rows):
+    for tile in range(TILES):
+        at = slice(BAND * tile, BAND * tile + BAND)
+        spans[tile] = far[at]
+        spans[7 * TILES + tile] = far[at]
+        for core in range(2):
+            for pair, source in enumerate((before, both, after)):
+                spans[(1 + 2 * pair + core) * TILES + tile] = source[core, at]
     weight_rows[...] = weights[...].T
     mine = weight_rows[pl.ds(pl.multiple_of(place_of(FEEDER_AXES) * BAND, BAND), BAND), :]
-    own_tile = edge + place_of(AXES[3:]) * TILES
+    own_tile = (HOPS + lax.axis_index("core")) * TILES
     own_column = own_tile * 128
     count = lags.shape[0]
     gains = [jnp.broadcast_to(mine[:, k : k + 1], (BAND, 128)) for k in range(count)]
@@ -254,24 +228,23 @@
         )
 
 
-def ar_terms(lags, weights, plane, beside, home):
+def ar_terms(lags, weights, before, both, after, far, home):
     in_vmem = pl.BlockSpec(memory_space=pltpu.VMEM)
     in_smem = pl.BlockSpec(memory_space=pltpu.SMEM)
-    tiles = (2 * HOPS + PLANE) * TILES
     return pl.pallas_call(
         ar_kernel,
-        in_specs=[in_smem] + [in_vmem] * 4,
+        in_specs=[in_smem] + [in_vmem] * 6,
         out_specs=in_vmem,
         out_shape=jax.ShapeDtypeStruct((BAND, SPAN), jnp.float32),
         scratch_shapes=[
-            pltpu.VMEM((tiles + 1, BAND, 128), jnp.float32),
+            pltpu.VMEM((2 * (HOPS + 1) * TILES + 1, BAND, 128), jnp.float32),
             pltpu.VMEM((CHUNKS + 1, BAND, 128), jnp.float32),
             pltpu.VMEM(weights.shape[::-1], jnp.float32),
         ],
         cost_estimate=pl.CostEstimate(flops=2_000_000, bytes_accessed=400_000, transcendentals=0),
         compiler_params=pltpu.CompilerParams(vmem_limit_bytes=8 << 20),
         name="ar_terms",
-    )(lags, weights, plane, beside, home)
+    )(lags, weights, before, both, after, far, home)
 
 
 def per_device(
@@ -280,23 +253,28 @@
     ranks = time_factor.shape[0]
     tm_place = lax.axis_index(TM_AXES)
 
-    keep, send, bands, sent_bands = main_terms(observed, mask_words.T, feeder_factor.T, time_factor)
+    keep, send, own_band, bands, sent_bands = main_terms(
+        observed, mask_words.T, feeder_factor.T, time_factor
+    )
     got = lax.ppermute(send, "core", [(0, 1), (1, 0)])
     own_factor = lax.dynamic_slice_in_dim(feeder_factor, tm_place * SHARE, SHARE, 0)
     bands = bands + lax.ppermute(sent_bands, "y", [(0, 1), (1, 0), (2, 3), (3, 2)])
-    pair = pair_terms(keep, got)
+    pair, both = on_chip(
+        pair_kernel, (keep, own_band, got), ((PLANE // 2, MAIN_ROWS, 128), (2, BAND_ROWS, 128))
+    )
     bands = bands[0] + lax.ppermute(bands[1], "y", [(0, 3), (3, 0), (1, 2), (2, 1)])
     got = lax.all_to_all(pair, "x", 0, 0, tiled=True)
     away = lax.ppermute(bands[1], "z_hi", [(0, 1), (1, 0)])
 
-    planes, passed = split_terms(got)
-    plane = got[:, MAIN_ROWS:].reshape(PLANE, BAND_ROWS, 128)
-    pairs = [(t, t + PLANE) for t in range(TM - PLANE) if t % PLANE < PLANE // 2]
-    pairs += [(t, t - PLANE) for t in range(PLANE, TM) if t % PLANE >= PLANE // 2]
-    beside = lax.ppermute(passed, TM_AXES, pairs)
+    before = lax.ppermute(both, TM_AXES, [(t, t + 2) for t in range(TM - 2)])
+    after = lax.ppermute(both, TM_AXES, [(t, t - 2) for t in range(2, TM)])
+    pairs = [(t, t + 3 if t % 2 else t - 3) for t in range(TM)]
+    far = lax.ppermute(own_band, TM_AXES, [(t, to) for t, to in pairs if 0 <= to < TM])
+    (planes,) = on_chip(sum_kernel, (got,), ((PLANES, SHARE // 2, 128),))
     share = lax.all_to_all(planes, "z_lo", 0, 0, tiled=True)
     share = share.sum(0)
-    time_grad = ar_terms(lags, ar_weight, plane, beside, bands[0]) + away
+    half_grad = ar_terms(lags, ar_weight, before, both, after, far, bands[0])
+    time_grad = half_grad + away
 
     grad_share = jnp.concatenate([share[:, :ranks], share[:, ranks:]], axis=0)
     factor_grad = grad_share + LAM_F * own_factor

time: 57.9 us -> 63.2 us (1.092)
  the two profiles are of different devices: /device:TPU:100 before, /device:TPU:102 now
where the time goes in v6:
time: 63.2 us; the launch traced here: 62.6 us
  starting transfers between devices  45 us (71%)
  Pallas kernels  8.22 us (13%)
  waiting for transfers between devices  6.21 us (10%)
  other arithmetic  1.28 us (2%)
  local copies, waits for them, and re-layouts  1.09 us (2%)
  between operations  0.81 us (1%)
    all_to_all x1, starting transfers between devices, per_device(): share = lax.all_to_all(planes, 'z_lo', 0, 0, tiled=True)  11.7 us
    ppermute x1, starting transfers between devices, per_device(): away = lax.ppermute(bands[1], 'z_hi', [(0, 1), (1, 0)])  8.22 us
    ppermute x1, starting transfers between devices, per_device(): before = lax.ppermute(both, TM_AXES, [(t, t + 2) for t in range(TM - 2)])  6.54 us
    ppermute x1, waiting for transfers between devices, per_device(): after = lax.ppermute(both, TM_AXES, [(t, t - 2) for t in range(2, TM)])  6.18 us
    pallas_call x1, Pallas kernels, main_terms(): pl.pallas_call(functools.partial(main_kernel, steps=steps, planes=PLANES...  5.75 us
    all_to_all x1, starting transfers between devices, per_device(): got = lax.all_to_all(pair, 'x', 0, 0, tiled=True)  4.76 us
    ppermute x1, starting transfers between devices, per_device(): lax.ppermute(bands[1], 'y', [(0, 3), (3, 0), (1, 2), (2, 1)])  4.09 us
    ppermute x1, starting transfers between devices, per_device(): lax.ppermute(sent_bands, 'y', [(0, 1), (1, 0), (2, 3), (3, 2)])  3.49 us
  transfers between devices with their start and end apart: 9, of which 1 were waited for; matrix products, arithmetic and copies ran while one was open for 3% of the time, Pallas kernels for 4%

profile of v6, /device:TPU:102, one launch (start us, length us, event | category | flops | bytes accessed | tf_op | source)
XLA Modules:
  0.0 62.6 jit_solution(11954794881933337551)
XLA Ops:
  0.6 0.0 copy-start
  0.6 0.0 copy-start.1
  0.7 0.0 copy-start.2
  0.7 0.0 copy-start.3
  0.7 5.7 %main_terms.1 = (f32[768,128]{1,0:T(8,128)S(1)}, f32[800,128]{1,0:T(8,128)S(1)}, f32[32,128]{1,0:T(8,128)S(1)}, f32[2,2,8,512]{3,2,1,0:T(8,128)S(1)}, f32[2,2,8,512]{3,2,1,0:T(8,128)S(1)}) custom-call(bf16[3072,512]{1,0:T(8,128)(2,1)} %observed.1, s32[64,3072]{1,0:T(8,128)} %bitcast.13, f32[64,3072]{1,0:T(8,128)} %bitcast.12, f32[64,512]{1,0:T(8,128)} %time.1), custom_call_target="tpu_custom_call" | custom-call | flops 805306368 | bytes 6000000 | tf_op jit(solution)/shard_map/main_terms/pallas_call | solution.py:124
  6.4 1.9 %collective-permute-start = (f32[800,128]{1,0:T(8,128)S(1)}, f32[800,128]{1,0:T(8,128)S(1)}, u32[]{:S(2)}, u32[]{:S(2)}) collective-permute-start(f32[800,128]{1,0:T(8,128)S(1)} %get-tuple-element.13), channel_id=1, source_target_pairs={{0,1},{1,0},{2,3},{3,2},{4,5},{5,4},{6,7},{7,6},{8,9},{9,8},{10,11... | collective-permute-start | bytes 1228808 | tf_op jit(solution)/shard_map/ppermute | solution.py:259
  8.4 3.5 %collective-permute-start.4 = (f32[2,2,8,512]{3,2,1,0:T(8,128)S(1)}, f32[2,2,8,512]{3,2,1,0:T(8,128)S(1)}, u32[]{:S(2)}, u32[]{:S(2)}) collective-permute-start(f32[2,2,8,512]{3,2,1,0:T(8,128)S(1)} %get-tuple-element.17), channel_id=1, source_target_pairs={{0,64},{64,0},{128,192},{192,128},{1,65},{65,1},{129,193},{193,129... | collective-permute-start | bytes 196616 | tf_op jit(solution)/shard_map/ppermute | solution.py:261
  11.9 0.0 collective-permute-done.got
  11.9 0.8 %shard_map.111 = (f32[4,192,128]{2,1,0:T(8,128)}, f32[2,32,128]{2,1,0:T(8,128)S(1)}) custom-call(f32[768,128]{1,0:T(8,128)S(1)} %get-tuple-element.11.keep, f32[32,128]{1,0:T(8,128)S(1)} %get-tuple-element.12.own_band, f32[800,128]{1,0:T(8,128)S(1)} %collective-permute-done.got), custom_call_target="tpu_custom_call" | custom-call | flops 100000 | bytes 1000000 | tf_op jit(solution)/shard_map/pallas_call | solution.py:175
  12.7 4.8 %all-to-all-start = ((f32[4,192,128]{2,1,0:T(8,128)}), f32[4,192,128]{2,1,0:T(8,128)S(1)}, u32[]{:S(2)}, u32[]{:S(2)}) async-start(f32[4,192,128]{2,1,0:T(8,128)} %get-tuple-element.14), calls=%async_computation | async-start | bytes 786432 | tf_op jit(solution)/shard_map/all_to_all | solution.py:266
  17.4 0.0 collective-permute-done.4
  17.5 4.1 %collective-permute-start.5 = (f32[2,8,512]{2,1,0:T(8,128)S(1)}, f32[2,8,512]{2,1,0:T(8,128)S(1)}, u32[]{:S(2)}, u32[]{:S(2)}) collective-permute-start(f32[2,8,512]{2,1,0:T(8,128)S(1)} %slice_bitcast_fusion), channel_id=1, source_target_pairs={{0,192},{192,0},{64,128},{128,64},{1,193},{193,1},{65,129},{129,65... | collective-permute-start | bytes 98312 | tf_op jit(solution)/shard_map/ppermute | solution.py:265
  21.6 2.4 %collective-permute-start.3 = (f32[32,128]{1,0:T(8,128)S(1)}, f32[32,128]{1,0:T(8,128)S(1)}, u32[]{:S(2)}, u32[]{:S(2)}) collective-permute-start(f32[32,128]{1,0:T(8,128)S(1)} %get-tuple-element.12.own_band), channel_id=1, source_target_pairs={{1,4},{3,6},{4,1},{5,8},{6,3},{7,10},{8,5},{9,12},{10,7},{11,14},{... | collective-permute-start | bytes 49160 | tf_op jit(solution)/shard_map/ppermute | solution.py:272
  23.9 0.0 all-to-all-done.got
  23.9 0.7 %shard_map.112 = f32[8,24,128]{2,1,0:T(8,128)} custom-call(f32[4,192,128]{2,1,0:T(8,128)S(1)} %all-to-all-done.got), custom_call_target="tpu_custom_call" | custom-call | flops 100000 | bytes 1000000 | tf_op jit(solution)/shard_map/pallas_call | solution.py:175
  24.6 11.7 %all-to-all-start.1 = ((f32[8,24,128]{2,1,0:T(8,128)}), f32[8,24,128]{2,1,0:T(8,128)S(1)}, u32[]{:S(2)}, u32[]{:S(2)}) async-start(f32[8,24,128]{2,1,0:T(8,128)} %shard_map.112), calls=%async_computation.1 | async-start | bytes 196608 | tf_op jit(solution)/shard_map/all_to_all | solution.py:274
  36.3 0.0 collective-permute-done.5
  36.4 8.2 %collective-permute-start.6 = (f32[8,512]{1,0:T(8,128)S(1)}, f32[8,512]{1,0:T(8,128)S(1)}, u32[]{:S(2)}, u32[]{:S(2)}) collective-permute-start(f32[8,512]{1,0:T(8,128)S(1)} %get-tuple-element.21), channel_id=1, source_target_pairs={{0,256},{256,0},{1,257},{257,1},{2,258},{258,2},{3,259},{259,3},{4... | collective-permute-start | bytes 49160 | tf_op jit(solution)/shard_map/ppermute | solution.py:267
  44.6 6.5 %collective-permute-start.1 = (f32[2,32,128]{2,1,0:T(8,128)S(1)}, f32[2,32,128]{2,1,0:T(8,128)S(1)}, u32[]{:S(2)}, u32[]{:S(2)}) collective-permute-start(f32[2,32,128]{2,1,0:T(8,128)S(1)} %get-tuple-element.15.both), channel_id=1, source_target_pairs={{0,2},{1,3},{2,4},{3,5},{4,6},{5,7},{6,8},{7,9},{8,10},{9,11},{10,... | collective-permute-start | bytes 98312 | tf_op jit(solution)/shard_map/ppermute | solution.py:269
  51.1 1.9 %collective-permute-start.2 = (f32[2,32,128]{2,1,0:T(8,128)S(1)}, f32[2,32,128]{2,1,0:T(8,128)S(1)}, u32[]{:S(2)}, u32[]{:S(2)}) collective-permute-start(f32[2,32,128]{2,1,0:T(8,128)S(1)} %get-tuple-element.15.both), channel_id=1, source_target_pairs={{2,0},{3,1},{4,2},{5,3},{6,4},{7,5},{8,6},{9,7},{10,8},{11,9},{12,... | collective-permute-start | bytes 98312 | tf_op jit(solution)/shard_map/ppermute | solution.py:270
  53.0 0.9 %constant_dynamic-slice_fusion = f32[48,64]{0,1:T(8,128)S(1)} fusion(f32[3072,64]{0,1:T(8,128)} %param.10, s32[]{:T(128)S(6)} %select_n.3), kind=kLoop, calls=%fused_computation.10 | loop fusion | bytes 24580 | tf_op jit(solution)/shard_map/dynamic_slice | solution.py:260
  54.0 0.1 copy.13
  54.0 0.0 collective-permute-done.3.far
  54.1 0.0 collective-permute-done.1.before
  54.1 6.2 %collective-permute-done.2.after = f32[2,32,128]{2,1,0:T(8,128)S(1)} collective-permute-done((f32[2,32,128]{2,1,0:T(8,128)S(1)}, f32[2,32,128]{2,1,0:T(8,128)S(1)}, u32[]{:S(2)}, u32[]{:S(2)}) %collective-permute-start.2) | collective-permute-done | bytes 32800 | tf_op jit(solution)/shard_map/ppermute | solution.py:270
  60.2 0.0 copy-done
  60.3 0.0 copy-done.1
  60.3 1.0 %ar_terms.1 = f32[8,512]{1,0:T(8,128)S(1)} custom-call(s32[10]{0:T(128)S(1)} %copy-done.1, f32[10,64]{1,0:T(8,128)S(1)} %copy-done, f32[2,32,128]{2,1,0:T(8,128)S(1)} %collective-permute-done.1.before, f32[2,32,128]{2,1,0:T(8,128)S(1)} %get-tuple-element.15.both, f32[2,32,128]{2,1,0:T(8,128)S(1)} %collective-permute-done.2.after, ...), custom_call_target="tpu_custom_call" | custom-call | flops 2000000 | bytes 400000 | tf_op jit(solution)/shard_map/ar_terms/pallas_call | solution.py:234
  61.3 0.0 collective-permute-done.6
  61.3 0.6 add.43
  61.9 0.0 all-to-all-done.1
  61.9 0.1 fusion.3
  62.0 0.0 copy-done.2
  62.0 0.0 copy-done.3
  62.0 0.6 %divide_subtract_fusion = (f32[48,64]{1,0:T(8,128)}, f32[48,64]{1,0:T(8,128)}, f32[48,64]{1,0:T(8,128)}) fusion(f32[48,64]{1,0:T(8,128)S(1)} %copy.13, f32[24,64]{1,0:T(8,128)S(1)} %get-tuple-element.24, f32[24,64]{1,0:T(8,128)S(1)} %get-tuple-element.23, f32[48,64]{1,0:T(8,128)S(1)} %copy-done.2, f32[48,64]{1,0:T(8,128)S(1)} %copy-done.3), kind=kLoop, calls=%fused_computation.6 | loop fusion | flops 46080 | bytes 86016 | tf_op jit(solution)/shard_map/sub | solution.py:286
  (5 shorter events, 0.0 us)
Async XLA Ops:
  0.6 59.6 %copy-start = (f32[10,64]{1,0:T(8,128)S(1)}, f32[10,64]{1,0:T(8,128)}, u32[]{:S(2)}) copy-start(f32[10,64]{1,0:T(8,128)} %weights.1) | copy-start | bytes 7684
  0.6 59.6 %copy-start.1 = (s32[10]{0:T(128)S(1)}, s32[10]{0:T(128)}, u32[]{:S(2)}) copy-start(s32[10]{0:T(128)} %lags.1) | copy-start | bytes 124
  0.7 61.3 %copy-start.2 = (f32[48,64]{1,0:T(8,128)S(1)}, f32[48,64]{1,0:T(8,128)}, u32[]{:S(2)}) copy-start(f32[48,64]{1,0:T(8,128)} %param.14) | copy-start | bytes 36868
  0.7 61.3 %copy-start.3 = (f32[48,64]{1,0:T(8,128)S(1)}, f32[48,64]{1,0:T(8,128)}, u32[]{:S(2)}) copy-start(f32[48,64]{1,0:T(8,128)} %param.15) | copy-start | bytes 36868
  6.4 5.4 %collective-permute-start = (f32[800,128]{1,0:T(8,128)S(1)}, f32[800,128]{1,0:T(8,128)S(1)}, u32[]{:S(2)}, u32[]{:S(2)}) collective-permute-start(f32[800,128]{1,0:T(8,128)S(1)} %get-tuple-element.13), channel_id=1, source_target_pairs={{0,1},{1,0},{2,3},{3,2},{4,5},{5,4},{6,7},{7,6},{8,9},{9,8},{10,11... | collective-permute-start | bytes 1228808 | tf_op jit(solution)/shard_map/ppermute | solution.py:259
  8.4 9.1 %collective-permute-start.4 = (f32[2,2,8,512]{3,2,1,0:T(8,128)S(1)}, f32[2,2,8,512]{3,2,1,0:T(8,128)S(1)}, u32[]{:S(2)}, u32[]{:S(2)}) collective-permute-start(f32[2,2,8,512]{3,2,1,0:T(8,128)S(1)} %get-tuple-element.17), channel_id=1, source_target_pairs={{0,64},{64,0},{128,192},{192,128},{1,65},{65,1},{129,193},{193,129... | collective-permute-start | bytes 196616 | tf_op jit(solution)/shard_map/ppermute | solution.py:261
  12.7 11.3 %all-to-all-start = ((f32[4,192,128]{2,1,0:T(8,128)}), f32[4,192,128]{2,1,0:T(8,128)S(1)}, u32[]{:S(2)}, u32[]{:S(2)}) async-start(f32[4,192,128]{2,1,0:T(8,128)} %get-tuple-element.14), calls=%async_computation | async-start | bytes 786432 | tf_op jit(solution)/shard_map/all_to_all | solution.py:266
  17.5 18.9 %collective-permute-start.5 = (f32[2,8,512]{2,1,0:T(8,128)S(1)}, f32[2,8,512]{2,1,0:T(8,128)S(1)}, u32[]{:S(2)}, u32[]{:S(2)}) collective-permute-start(f32[2,8,512]{2,1,0:T(8,128)S(1)} %slice_bitcast_fusion), channel_id=1, source_target_pairs={{0,192},{192,0},{64,128},{128,64},{1,193},{193,1},{65,129},{129,65... | collective-permute-start | bytes 98312 | tf_op jit(solution)/shard_map/ppermute | solution.py:265
  21.6 32.5 %collective-permute-start.3 = (f32[32,128]{1,0:T(8,128)S(1)}, f32[32,128]{1,0:T(8,128)S(1)}, u32[]{:S(2)}, u32[]{:S(2)}) collective-permute-start(f32[32,128]{1,0:T(8,128)S(1)} %get-tuple-element.12.own_band), channel_id=1, source_target_pairs={{1,4},{3,6},{4,1},{5,8},{6,3},{7,10},{8,5},{9,12},{10,7},{11,14},{... | collective-permute-start | bytes 49160 | tf_op jit(solution)/shard_map/ppermute | solution.py:272
  24.6 37.3 %all-to-all-start.1 = ((f32[8,24,128]{2,1,0:T(8,128)}), f32[8,24,128]{2,1,0:T(8,128)S(1)}, u32[]{:S(2)}, u32[]{:S(2)}) async-start(f32[8,24,128]{2,1,0:T(8,128)} %shard_map.112), calls=%async_computation.1 | async-start | bytes 196608 | tf_op jit(solution)/shard_map/all_to_all | solution.py:274
  36.4 24.9 %collective-permute-start.6 = (f32[8,512]{1,0:T(8,128)S(1)}, f32[8,512]{1,0:T(8,128)S(1)}, u32[]{:S(2)}, u32[]{:S(2)}) collective-permute-start(f32[8,512]{1,0:T(8,128)S(1)} %get-tuple-element.21), channel_id=1, source_target_pairs={{0,256},{256,0},{1,257},{257,1},{2,258},{258,2},{3,259},{259,3},{4... | collective-permute-start | bytes 49160 | tf_op jit(solution)/shard_map/ppermute | solution.py:267
  44.6 9.5 %collective-permute-start.1 = (f32[2,32,128]{2,1,0:T(8,128)S(1)}, f32[2,32,128]{2,1,0:T(8,128)S(1)}, u32[]{:S(2)}, u32[]{:S(2)}) collective-permute-start(f32[2,32,128]{2,1,0:T(8,128)S(1)} %get-tuple-element.15.both), channel_id=1, source_target_pairs={{0,2},{1,3},{2,4},{3,5},{4,6},{5,7},{6,8},{7,9},{8,10},{9,11},{10,... | collective-permute-start | bytes 98312 | tf_op jit(solution)/shard_map/ppermute | solution.py:269
  51.1 9.1 %collective-permute-start.2 = (f32[2,32,128]{2,1,0:T(8,128)S(1)}, f32[2,32,128]{2,1,0:T(8,128)S(1)}, u32[]{:S(2)}, u32[]{:S(2)}) collective-permute-start(f32[2,32,128]{2,1,0:T(8,128)S(1)} %get-tuple-element.15.both), channel_id=1, source_target_pairs={{2,0},{3,1},{4,2},{5,3},{6,4},{7,5},{8,6},{9,7},{10,8},{11,9},{12,... | collective-permute-start | bytes 98312 | tf_op jit(solution)/shard_map/ppermute | solution.py:270

commit v7 on v5

--- a/solution.py
+++ b/solution.py
@@ -118,7 +118,7 @@
                     time_keep[near >> 1, z] = rows_out
 
 
-def main_terms(observed, words, factor, time, steps=4):
+def main_terms(observed, words, factor, time, steps=2):
     feeders, span = observed.shape
     ranks, block = factor.shape[0], feeders // steps
     half_rows = PLANE // 2 * MAIN_ROWS + BAND_ROWS
@@ -296,7 +296,8 @@
     beside = lax.ppermute(passed, TM_AXES, pairs)
     share = lax.all_to_all(planes, "z_lo", 0, 0, tiled=True)
     share = share.sum(0)
-    time_grad = ar_terms(lags, ar_weight, plane, beside, bands[0]) + away
+    half_grad = ar_terms(lags, ar_weight, plane, beside, bands[0])
+    time_grad = half_grad + away
 
     grad_share = jnp.concatenate([share[:, :ranks], share[:, ranks:]], axis=0)
     factor_grad = grad_share + LAM_F * own_factor
@@ -305,7 +306,8 @@
     update = (
         LEARNING_RATE * (new_first / BIAS_FIRST) / (jnp.sqrt(new_second / BIAS_SECOND) + ADAM_EPS)
     )
-    return (own_factor - update, new_first, new_second, time_grad)
+    new_factor = own_factor - update
+    return (new_factor, new_first, new_second, time_grad)
 
 
 def solution(mesh):

time: 57.9 us -> 57.4 us (level)
  no operation moved by 1% of the time
where the time goes in v7:
time: 57.4 us; the launch traced here: 56.9 us
  starting transfers between devices  37.7 us (66%)
  waiting for transfers between devices  8.26 us (14%)
  Pallas kernels  7.82 us (14%)
  other arithmetic  1.28 us (2%)
  local copies, waits for them, and re-layouts  1.12 us (2%)
  between operations  0.78 us (1%)
    all_to_all x1, starting transfers between devices, per_device(): share = lax.all_to_all(planes, 'z_lo', 0, 0, tiled=True)  11.7 us
    ppermute x1, starting transfers between devices, per_device(): away = lax.ppermute(bands[1], 'z_hi', [(0, 1), (1, 0)])  8.22 us
    pallas_call x1, Pallas kernels, main_terms(): pl.pallas_call(functools.partial(main_kernel, steps=steps, planes=PLANES...  5.31 us
    ppermute x1, starting transfers between devices, per_device(): lax.ppermute(bands[1], 'y', [(0, 3), (3, 0), (1, 2), (2, 1)])  4.92 us
    all_to_all x1, starting transfers between devices, per_device(): got = lax.all_to_all(pair, 'x', 0, 0, tiled=True)  4.8 us
    ppermute x1, waiting for transfers between devices, per_device(): beside = lax.ppermute(passed, TM_AXES, pairs)  3.87 us
    ppermute x1, starting transfers between devices, per_device(): lax.ppermute(sent_bands, 'y', [(0, 1), (1, 0), (2, 3), (3, 2)])  3.47 us
    ppermute x1, waiting for transfers between devices, per_device(): lax.ppermute(sent_bands, 'y', [(0, 1), (1, 0), (2, 3), (3, 2)])  2.67 us
  transfers between devices with their start and end apart: 7, of which 3 were waited for; matrix products, arithmetic and copies ran while one was open for 3% of the time, Pallas kernels for 3%

profile of v7, /device:TPU:100, one launch (start us, length us, event | category | flops | bytes accessed | tf_op | source)
XLA Modules:
  0.0 56.9 jit_solution(5544366309246182133)
XLA Ops:
  0.6 5.3 %main_terms.1 = (f32[800,128]{1,0:T(8,128)S(1)}, f32[800,128]{1,0:T(8,128)S(1)}, f32[2,2,8,512]{3,2,1,0:T(8,128)S(1)}, f32[2,2,8,512]{3,2,1,0:T(8,128)S(1)}) custom-call(bf16[3072,512]{1,0:T(8,128)(2,1)} %observed.1, s32[64,3072]{1,0:T(8,128)} %bitcast.15, f32[64,3072]{1,0:T(8,128)} %bitcast.14, f32[64,512]{1,0:T(8,128)} %time.1), custom_call_target="tpu_custom_call" | custom-call | flops 805306368 | bytes 6000000 | tf_op jit(solution)/shard_map/main_terms/pallas_call | solution.py:125
  5.9 0.0 copy-start
  6.0 0.0 copy-start.1
  6.0 0.0 copy-start.2
  6.0 0.0 copy-start.3
  6.0 2.1 %collective-permute-start = (f32[800,128]{1,0:T(8,128)S(1)}, f32[800,128]{1,0:T(8,128)S(1)}, u32[]{:S(2)}, u32[]{:S(2)}) collective-permute-start(f32[800,128]{1,0:T(8,128)S(1)} %get-tuple-element.11), channel_id=1, source_target_pairs={{0,1},{1,0},{2,3},{3,2},{4,5},{5,4},{6,7},{7,6},{8,9},{9,8},{10,11... | collective-permute-start | bytes 1228808 | tf_op jit(solution)/shard_map/ppermute | solution.py:284
  8.1 1.7 %collective-permute-done.got = f32[800,128]{1,0:T(8,128)S(1)} collective-permute-done((f32[800,128]{1,0:T(8,128)S(1)}, f32[800,128]{1,0:T(8,128)S(1)}, u32[]{:S(2)}, u32[]{:S(2)}) %collective-permute-start) | collective-permute-done | bytes 409632 | tf_op jit(solution)/shard_map/ppermute | solution.py:284
  9.8 0.8 %pair_terms.1 = f32[4,256,128]{2,1,0:T(8,128)} custom-call(f32[800,128]{1,0:T(8,128)S(1)} %get-tuple-element.10.keep, f32[800,128]{1,0:T(8,128)S(1)} %collective-permute-done.got), custom_call_target="tpu_custom_call" | custom-call | flops 100000 | bytes 1400000 | tf_op jit(solution)/shard_map/pair_terms/pallas_call | solution.py:166
  10.6 4.8 %all-to-all-start = ((f32[4,256,128]{2,1,0:T(8,128)}), f32[4,256,128]{2,1,0:T(8,128)S(1)}, u32[]{:S(2)}, u32[]{:S(2)}) async-start(f32[4,256,128]{2,1,0:T(8,128)} %pair_terms.1), calls=%async_computation | async-start | bytes 1048576 | tf_op jit(solution)/shard_map/all_to_all | solution.py:289
  15.4 3.5 %collective-permute-start.2 = (f32[2,2,8,512]{3,2,1,0:T(8,128)S(1)}, f32[2,2,8,512]{3,2,1,0:T(8,128)S(1)}, u32[]{:S(2)}, u32[]{:S(2)}) collective-permute-start(f32[2,2,8,512]{3,2,1,0:T(8,128)S(1)} %get-tuple-element.15), channel_id=1, source_target_pairs={{0,64},{64,0},{128,192},{192,128},{1,65},{65,1},{129,193},{193,129... | collective-permute-start | bytes 196616 | tf_op jit(solution)/shard_map/ppermute | solution.py:286
  18.9 2.7 %collective-permute-done.2 = f32[2,2,8,512]{3,2,1,0:T(8,128)S(1)} collective-permute-done((f32[2,2,8,512]{3,2,1,0:T(8,128)S(1)}, f32[2,2,8,512]{3,2,1,0:T(8,128)S(1)}, u32[]{:S(2)}, u32[]{:S(2)}) %collective-permute-start.2) | collective-permute-done | bytes 65568 | tf_op jit(solution)/shard_map/ppermute | solution.py:286
  21.6 4.9 %collective-permute-start.3 = (f32[2,8,512]{2,1,0:T(8,128)S(1)}, f32[2,8,512]{2,1,0:T(8,128)S(1)}, u32[]{:S(2)}, u32[]{:S(2)}) collective-permute-start(f32[2,8,512]{2,1,0:T(8,128)S(1)} %slice_bitcast_fusion), channel_id=1, source_target_pairs={{0,192},{192,0},{64,128},{128,64},{1,193},{193,1},{65,129},{129,65... | collective-permute-start | bytes 98312 | tf_op jit(solution)/shard_map/ppermute | solution.py:288
  26.5 0.0 all-to-all-done.got
  26.5 0.7 %split_terms.1 = (f32[8,24,128]{2,1,0:T(8,128)}, f32[3,32,128]{2,1,0:T(8,128)S(1)}) custom-call(f32[4,256,128]{2,1,0:T(8,128)S(1)} %all-to-all-done.got), custom_call_target="tpu_custom_call" | custom-call | flops 100000 | bytes 700000 | tf_op jit(solution)/shard_map/split_terms/pallas_call | solution.py:195
  27.2 11.7 %all-to-all-start.1 = ((f32[8,24,128]{2,1,0:T(8,128)}), f32[8,24,128]{2,1,0:T(8,128)S(1)}, u32[]{:S(2)}, u32[]{:S(2)}) async-start(f32[8,24,128]{2,1,0:T(8,128)} %get-tuple-element.12), calls=%async_computation.1 | async-start | bytes 196608 | tf_op jit(solution)/shard_map/all_to_all | solution.py:297
  38.9 0.0 collective-permute-done.3
  38.9 8.2 %collective-permute-start.4 = (f32[8,512]{1,0:T(8,128)S(1)}, f32[8,512]{1,0:T(8,128)S(1)}, u32[]{:S(2)}, u32[]{:S(2)}) collective-permute-start(f32[8,512]{1,0:T(8,128)S(1)} %get-tuple-element.19), channel_id=1, source_target_pairs={{0,256},{256,0},{1,257},{257,1},{2,258},{258,2},{3,259},{259,3},{4... | collective-permute-start | bytes 49160 | tf_op jit(solution)/shard_map/ppermute | solution.py:290
  47.2 2.5 %collective-permute-start.1 = (f32[3,32,128]{2,1,0:T(8,128)S(1)}, f32[3,32,128]{2,1,0:T(8,128)S(1)}, u32[]{:S(2)}, u32[]{:S(2)}) collective-permute-start(f32[3,32,128]{2,1,0:T(8,128)S(1)} %get-tuple-element.13), channel_id=1, source_target_pairs={{0,8},{1,9},{2,10},{3,11},{8,16},{9,17},{10,18},{11,19},{16,24},{1... | collective-permute-start | bytes 147464 | tf_op jit(solution)/shard_map/ppermute | solution.py:296
  49.6 0.9 %constant_dynamic-slice_fusion = f32[48,64]{0,1:T(8,128)S(1)} fusion(f32[3072,64]{0,1:T(8,128)} %param.10, s32[]{:T(128)S(6)} %select_n.3), kind=kLoop, calls=%fused_computation.10 | loop fusion | bytes 24580 | tf_op jit(solution)/shard_map/dynamic_slice | solution.py:285
  50.6 0.1 copy.13
  50.7 3.9 %collective-permute-done.1.beside = f32[3,32,128]{2,1,0:T(8,128)S(1)} collective-permute-done((f32[3,32,128]{2,1,0:T(8,128)S(1)}, f32[3,32,128]{2,1,0:T(8,128)S(1)}, u32[]{:S(2)}, u32[]{:S(2)}) %collective-permute-start.1) | collective-permute-done | bytes 49184 | tf_op jit(solution)/shard_map/ppermute | solution.py:296
  54.5 0.0 copy-done
  54.5 0.0 copy-done.1
  54.5 1.0 %ar_terms.1 = f32[8,512]{1,0:T(8,128)S(1)} custom-call(s32[10]{0:T(128)S(1)} %copy-done.1, f32[10,64]{1,0:T(8,128)S(1)} %copy-done, f32[8,32,128]{2,1,0:T(8,128)S(1)} %bitcast.13, f32[3,32,128]{2,1,0:T(8,128)S(1)} %collective-permute-done.1.beside, f32[8,512]{1,0:T(8,128)S(1)} %get-tuple-element.20.home), custom_call_target="tpu_custom_call" | custom-call | flops 2000000 | bytes 400000 | tf_op jit(solution)/shard_map/ar_terms/pallas_call | solution.py:261
  55.6 0.0 collective-permute-done.4
  55.6 0.6 %add.43 = f32[8,512]{1,0:T(8,128)} add(f32[8,512]{1,0:T(8,128)S(1)} %ar_terms.1, f32[8,512]{1,0:T(8,128)S(1)} %collective-permute-done.4) | non-fusion elementwise | flops 4096 | bytes 49152 | tf_op jit(solution)/shard_map/add | solution.py:300
  56.2 0.0 all-to-all-done.1
  56.2 0.1 fusion.3
  56.3 0.0 copy-done.2
  56.3 0.0 copy-done.3
  56.3 0.6 %divide_subtract_fusion = (f32[48,64]{1,0:T(8,128)}, f32[48,64]{1,0:T(8,128)}, f32[48,64]{1,0:T(8,128)}) fusion(f32[48,64]{1,0:T(8,128)S(1)} %copy.13, f32[24,64]{1,0:T(8,128)S(1)} %get-tuple-element.22, f32[24,64]{1,0:T(8,128)S(1)} %get-tuple-element.21, f32[48,64]{1,0:T(8,128)S(1)} %copy-done.2, f32[48,64]{1,0:T(8,128)S(1)} %copy-done.3), kind=kLoop, calls=%fused_computation.6 | loop fusion | flops 46080 | bytes 86016 | tf_op jit(solution)/shard_map/sub | solution.py:309
  (6 shorter events, 0.1 us)
Async XLA Ops:
  5.9 48.6 %copy-start = (f32[10,64]{1,0:T(8,128)S(1)}, f32[10,64]{1,0:T(8,128)}, u32[]{:S(2)}) copy-start(f32[10,64]{1,0:T(8,128)} %weights.1) | copy-start | bytes 7684
  6.0 48.6 %copy-start.1 = (s32[10]{0:T(128)S(1)}, s32[10]{0:T(128)}, u32[]{:S(2)}) copy-start(s32[10]{0:T(128)} %lags.1) | copy-start | bytes 124
  6.0 50.3 %copy-start.2 = (f32[48,64]{1,0:T(8,128)S(1)}, f32[48,64]{1,0:T(8,128)}, u32[]{:S(2)}) copy-start(f32[48,64]{1,0:T(8,128)} %param.14) | copy-start | bytes 36868
  6.0 50.3 %copy-start.3 = (f32[48,64]{1,0:T(8,128)S(1)}, f32[48,64]{1,0:T(8,128)}, u32[]{:S(2)}) copy-start(f32[48,64]{1,0:T(8,128)} %param.15) | copy-start | bytes 36868
  6.0 3.8 %collective-permute-start = (f32[800,128]{1,0:T(8,128)S(1)}, f32[800,128]{1,0:T(8,128)S(1)}, u32[]{:S(2)}, u32[]{:S(2)}) collective-permute-start(f32[800,128]{1,0:T(8,128)S(1)} %get-tuple-element.11), channel_id=1, source_target_pairs={{0,1},{1,0},{2,3},{3,2},{4,5},{5,4},{6,7},{7,6},{8,9},{9,8},{10,11... | collective-permute-start | bytes 1228808 | tf_op jit(solution)/shard_map/ppermute | solution.py:284
  10.6 15.9 %all-to-all-start = ((f32[4,256,128]{2,1,0:T(8,128)}), f32[4,256,128]{2,1,0:T(8,128)S(1)}, u32[]{:S(2)}, u32[]{:S(2)}) async-start(f32[4,256,128]{2,1,0:T(8,128)} %pair_terms.1), calls=%async_computation | async-start | bytes 1048576 | tf_op jit(solution)/shard_map/all_to_all | solution.py:289
  15.4 6.1 %collective-permute-start.2 = (f32[2,2,8,512]{3,2,1,0:T(8,128)S(1)}, f32[2,2,8,512]{3,2,1,0:T(8,128)S(1)}, u32[]{:S(2)}, u32[]{:S(2)}) collective-permute-start(f32[2,2,8,512]{3,2,1,0:T(8,128)S(1)} %get-tuple-element.15), channel_id=1, source_target_pairs={{0,64},{64,0},{128,192},{192,128},{1,65},{65,1},{129,193},{193,129... | collective-permute-start | bytes 196616 | tf_op jit(solution)/shard_map/ppermute | solution.py:286
  21.6 17.3 %collective-permute-start.3 = (f32[2,8,512]{2,1,0:T(8,128)S(1)}, f32[2,8,512]{2,1,0:T(8,128)S(1)}, u32[]{:S(2)}, u32[]{:S(2)}) collective-permute-start(f32[2,8,512]{2,1,0:T(8,128)S(1)} %slice_bitcast_fusion), channel_id=1, source_target_pairs={{0,192},{192,0},{64,128},{128,64},{1,193},{193,1},{65,129},{129,65... | collective-permute-start | bytes 98312 | tf_op jit(solution)/shard_map/ppermute | solution.py:288
  27.2 29.0 %all-to-all-start.1 = ((f32[8,24,128]{2,1,0:T(8,128)}), f32[8,24,128]{2,1,0:T(8,128)S(1)}, u32[]{:S(2)}, u32[]{:S(2)}) async-start(f32[8,24,128]{2,1,0:T(8,128)} %get-tuple-element.12), calls=%async_computation.1 | async-start | bytes 196608 | tf_op jit(solution)/shard_map/all_to_all | solution.py:297
  38.9 16.6 %collective-permute-start.4 = (f32[8,512]{1,0:T(8,128)S(1)}, f32[8,512]{1,0:T(8,128)S(1)}, u32[]{:S(2)}, u32[]{:S(2)}) collective-permute-start(f32[8,512]{1,0:T(8,128)S(1)} %get-tuple-element.19), channel_id=1, source_target_pairs={{0,256},{256,0},{1,257},{257,1},{2,258},{258,2},{3,259},{259,3},{4... | collective-permute-start | bytes 49160 | tf_op jit(solution)/shard_map/ppermute | solution.py:290
  47.2 7.4 %collective-permute-start.1 = (f32[3,32,128]{2,1,0:T(8,128)S(1)}, f32[3,32,128]{2,1,0:T(8,128)S(1)}, u32[]{:S(2)}, u32[]{:S(2)}) collective-permute-start(f32[3,32,128]{2,1,0:T(8,128)S(1)} %get-tuple-element.13), channel_id=1, source_target_pairs={{0,8},{1,9},{2,10},{3,11},{8,16},{9,17},{10,18},{11,19},{16,24},{1... | collective-permute-start | bytes 147464 | tf_op jit(solution)/shard_map/ppermute | solution.py:296

commit v8 on v7

--- a/solution.py
+++ b/solution.py
@@ -230,17 +230,18 @@
     own_column = own_tile * 128
     count = lags.shape[0]
     gains = [jnp.broadcast_to(mine[:, k : k + 1], (BAND, 128)) for k in range(count)]
-    parts = [jnp.zeros((BAND, 128), jnp.float32) for _ in range(CHUNKS)]
-    for k in range(count):
-        moved = shifted_tiles(own_column - lags[k], CHUNKS, lambda i: spans[i])
-        parts = [part + gains[k] * tile for part, tile in zip(parts, moved)]
     lane = lax.broadcasted_iota(jnp.int32, (BAND, 128), 1)
     first = place_of(TM_AXES) * SPAN
-    for chunk in range(CHUNKS):
-        column = first + 128 * chunk + lane
-        inside = (column >= LAGMAX) & (column < TM * SPAN)
-        errors[chunk] = jnp.where(inside, spans[own_tile + chunk] - parts[chunk], 0.0)
-    errors[CHUNKS] = jnp.zeros((BAND, 128), jnp.float32)
+    for begin, end in ((0, TILES + 1), (LAGMAX >> 7, CHUNKS)):
+        parts = [jnp.zeros((BAND, 128), jnp.float32) for _ in range(begin, end)]
+        for k in range(count):
+            start = own_column + 128 * begin - lags[k]
+            moved = shifted_tiles(start, end - begin, lambda i: spans[i])
+            parts = [part + gains[k] * tile for part, tile in zip(parts, moved)]
+        for chunk, part in zip(range(begin, end), parts):
+            column = first + 128 * chunk + lane
+            inside = (column >= LAGMAX) & (column < TM * SPAN)
+            errors[chunk] = jnp.where(inside, spans[own_tile + chunk] - part, 0.0)
     carried = [jnp.zeros((BAND, 128), jnp.float32) for _ in range(TILES)]
     for k in range(count):
         moved = shifted_tiles(lags[k], TILES, lambda i: errors[i])
@@ -265,7 +266,7 @@
         out_shape=jax.ShapeDtypeStruct((BAND, SPAN), jnp.float32),
         scratch_shapes=[
             pltpu.VMEM((tiles + 1, BAND, 128), jnp.float32),
-            pltpu.VMEM((CHUNKS + 1, BAND, 128), jnp.float32),
+            pltpu.VMEM((CHUNKS, BAND, 128), jnp.float32),
             pltpu.VMEM(weights.shape[::-1], jnp.float32),
         ],
         cost_estimate=pl.CostEstimate(flops=2_000_000, bytes_accessed=400_000, transcendentals=0),

time: 57.4 us -> 57.3 us (level)
  no operation moved by 1% of the time
where the time goes in v8:
time: 57.3 us; the launch traced here: 56.9 us
  starting transfers between devices  37.7 us (66%)
  waiting for transfers between devices  8.26 us (14%)
  Pallas kernels  7.76 us (14%)
  other arithmetic  1.28 us (2%)
  local copies, waits for them, and re-layouts  1.12 us (2%)
  between operations  0.78 us (1%)
    all_to_all x1, starting transfers between devices, per_device(): share = lax.all_to_all(planes, 'z_lo', 0, 0, tiled=True)  11.7 us
    ppermute x1, starting transfers between devices, per_device(): away = lax.ppermute(bands[1], 'z_hi', [(0, 1), (1, 0)])  8.22 us
    pallas_call x1, Pallas kernels, main_terms(): pl.pallas_call(functools.partial(main_kernel, steps=steps, planes=PLANES...  5.31 us
    ppermute x1, starting transfers between devices, per_device(): lax.ppermute(bands[1], 'y', [(0, 3), (3, 0), (1, 2), (2, 1)])  4.92 us
    all_to_all x1, starting transfers between devices, per_device(): got = lax.all_to_all(pair, 'x', 0, 0, tiled=True)  4.8 us
    ppermute x1, waiting for transfers between devices, per_device(): beside = lax.ppermute(passed, TM_AXES, pairs)  3.87 us
    ppermute x1, starting transfers between devices, per_device(): lax.ppermute(sent_bands, 'y', [(0, 1), (1, 0), (2, 3), (3, 2)])  3.47 us
    ppermute x1, waiting for transfers between devices, per_device(): lax.ppermute(sent_bands, 'y', [(0, 1), (1, 0), (2, 3), (3, 2)])  2.67 us
  transfers between devices with their start and end apart: 7, of which 3 were waited for; matrix products, arithmetic and copies ran while one was open for 3% of the time, Pallas kernels for 3%

profile of v8, /device:TPU:100, one launch (start us, length us, event | category | flops | bytes accessed | tf_op | source)
XLA Modules:
  0.0 56.9 jit_solution(17225100837804829905)
XLA Ops:
  0.6 5.3 %main_terms.1 = (f32[800,128]{1,0:T(8,128)S(1)}, f32[800,128]{1,0:T(8,128)S(1)}, f32[2,2,8,512]{3,2,1,0:T(8,128)S(1)}, f32[2,2,8,512]{3,2,1,0:T(8,128)S(1)}) custom-call(bf16[3072,512]{1,0:T(8,128)(2,1)} %observed.1, s32[64,3072]{1,0:T(8,128)} %bitcast.15, f32[64,3072]{1,0:T(8,128)} %bitcast.14, f32[64,512]{1,0:T(8,128)} %time.1), custom_call_target="tpu_custom_call" | custom-call | flops 805306368 | bytes 6000000 | tf_op jit(solution)/shard_map/main_terms/pallas_call | solution.py:125
  5.9 0.0 copy-start
  6.0 0.0 copy-start.1
  6.0 0.0 copy-start.2
  6.0 0.0 copy-start.3
  6.0 2.1 %collective-permute-start = (f32[800,128]{1,0:T(8,128)S(1)}, f32[800,128]{1,0:T(8,128)S(1)}, u32[]{:S(2)}, u32[]{:S(2)}) collective-permute-start(f32[800,128]{1,0:T(8,128)S(1)} %get-tuple-element.11), channel_id=1, source_target_pairs={{0,1},{1,0},{2,3},{3,2},{4,5},{5,4},{6,7},{7,6},{8,9},{9,8},{10,11... | collective-permute-start | bytes 1228808 | tf_op jit(solution)/shard_map/ppermute | solution.py:285
  8.1 1.7 %collective-permute-done.got = f32[800,128]{1,0:T(8,128)S(1)} collective-permute-done((f32[800,128]{1,0:T(8,128)S(1)}, f32[800,128]{1,0:T(8,128)S(1)}, u32[]{:S(2)}, u32[]{:S(2)}) %collective-permute-start) | collective-permute-done | bytes 409632 | tf_op jit(solution)/shard_map/ppermute | solution.py:285
  9.8 0.8 %pair_terms.1 = f32[4,256,128]{2,1,0:T(8,128)} custom-call(f32[800,128]{1,0:T(8,128)S(1)} %get-tuple-element.10.keep, f32[800,128]{1,0:T(8,128)S(1)} %collective-permute-done.got), custom_call_target="tpu_custom_call" | custom-call | flops 100000 | bytes 1400000 | tf_op jit(solution)/shard_map/pair_terms/pallas_call | solution.py:166
  10.6 4.8 %all-to-all-start = ((f32[4,256,128]{2,1,0:T(8,128)}), f32[4,256,128]{2,1,0:T(8,128)S(1)}, u32[]{:S(2)}, u32[]{:S(2)}) async-start(f32[4,256,128]{2,1,0:T(8,128)} %pair_terms.1), calls=%async_computation | async-start | bytes 1048576 | tf_op jit(solution)/shard_map/all_to_all | solution.py:290
  15.4 3.5 %collective-permute-start.2 = (f32[2,2,8,512]{3,2,1,0:T(8,128)S(1)}, f32[2,2,8,512]{3,2,1,0:T(8,128)S(1)}, u32[]{:S(2)}, u32[]{:S(2)}) collective-permute-start(f32[2,2,8,512]{3,2,1,0:T(8,128)S(1)} %get-tuple-element.15), channel_id=1, source_target_pairs={{0,64},{64,0},{128,192},{192,128},{1,65},{65,1},{129,193},{193,129... | collective-permute-start | bytes 196616 | tf_op jit(solution)/shard_map/ppermute | solution.py:287
  18.9 2.7 %collective-permute-done.2 = f32[2,2,8,512]{3,2,1,0:T(8,128)S(1)} collective-permute-done((f32[2,2,8,512]{3,2,1,0:T(8,128)S(1)}, f32[2,2,8,512]{3,2,1,0:T(8,128)S(1)}, u32[]{:S(2)}, u32[]{:S(2)}) %collective-permute-start.2) | collective-permute-done | bytes 65568 | tf_op jit(solution)/shard_map/ppermute | solution.py:287
  21.6 4.9 %collective-permute-start.3 = (f32[2,8,512]{2,1,0:T(8,128)S(1)}, f32[2,8,512]{2,1,0:T(8,128)S(1)}, u32[]{:S(2)}, u32[]{:S(2)}) collective-permute-start(f32[2,8,512]{2,1,0:T(8,128)S(1)} %slice_bitcast_fusion), channel_id=1, source_target_pairs={{0,192},{192,0},{64,128},{128,64},{1,193},{193,1},{65,129},{129,65... | collective-permute-start | bytes 98312 | tf_op jit(solution)/shard_map/ppermute | solution.py:289
  26.5 0.0 all-to-all-done.got
  26.5 0.7 %split_terms.1 = (f32[8,24,128]{2,1,0:T(8,128)}, f32[3,32,128]{2,1,0:T(8,128)S(1)}) custom-call(f32[4,256,128]{2,1,0:T(8,128)S(1)} %all-to-all-done.got), custom_call_target="tpu_custom_call" | custom-call | flops 100000 | bytes 700000 | tf_op jit(solution)/shard_map/split_terms/pallas_call | solution.py:195
  27.2 11.7 %all-to-all-start.1 = ((f32[8,24,128]{2,1,0:T(8,128)}), f32[8,24,128]{2,1,0:T(8,128)S(1)}, u32[]{:S(2)}, u32[]{:S(2)}) async-start(f32[8,24,128]{2,1,0:T(8,128)} %get-tuple-element.12), calls=%async_computation.1 | async-start | bytes 196608 | tf_op jit(solution)/shard_map/all_to_all | solution.py:298
  38.9 0.0 collective-permute-done.3
  38.9 8.2 %collective-permute-start.4 = (f32[8,512]{1,0:T(8,128)S(1)}, f32[8,512]{1,0:T(8,128)S(1)}, u32[]{:S(2)}, u32[]{:S(2)}) collective-permute-start(f32[8,512]{1,0:T(8,128)S(1)} %get-tuple-element.19), channel_id=1, source_target_pairs={{0,256},{256,0},{1,257},{257,1},{2,258},{258,2},{3,259},{259,3},{4... | collective-permute-start | bytes 49160 | tf_op jit(solution)/shard_map/ppermute | solution.py:291
  47.2 2.5 %collective-permute-start.1 = (f32[3,32,128]{2,1,0:T(8,128)S(1)}, f32[3,32,128]{2,1,0:T(8,128)S(1)}, u32[]{:S(2)}, u32[]{:S(2)}) collective-permute-start(f32[3,32,128]{2,1,0:T(8,128)S(1)} %get-tuple-element.13), channel_id=1, source_target_pairs={{0,8},{1,9},{2,10},{3,11},{8,16},{9,17},{10,18},{11,19},{16,24},{1... | collective-permute-start | bytes 147464 | tf_op jit(solution)/shard_map/ppermute | solution.py:297
  49.6 0.9 %constant_dynamic-slice_fusion = f32[48,64]{0,1:T(8,128)S(1)} fusion(f32[3072,64]{0,1:T(8,128)} %param.10, s32[]{:T(128)S(6)} %select_n.3), kind=kLoop, calls=%fused_computation.10 | loop fusion | bytes 24580 | tf_op jit(solution)/shard_map/dynamic_slice | solution.py:286
  50.6 0.1 copy.13
  50.7 3.9 %collective-permute-done.1.beside = f32[3,32,128]{2,1,0:T(8,128)S(1)} collective-permute-done((f32[3,32,128]{2,1,0:T(8,128)S(1)}, f32[3,32,128]{2,1,0:T(8,128)S(1)}, u32[]{:S(2)}, u32[]{:S(2)}) %collective-permute-start.1) | collective-permute-done | bytes 49184 | tf_op jit(solution)/shard_map/ppermute | solution.py:297
  54.5 0.0 copy-done
  54.5 0.0 copy-done.1
  54.5 1.0 %ar_terms.1 = f32[8,512]{1,0:T(8,128)S(1)} custom-call(s32[10]{0:T(128)S(1)} %copy-done.1, f32[10,64]{1,0:T(8,128)S(1)} %copy-done, f32[8,32,128]{2,1,0:T(8,128)S(1)} %bitcast.13, f32[3,32,128]{2,1,0:T(8,128)S(1)} %collective-permute-done.1.beside, f32[8,512]{1,0:T(8,128)S(1)} %get-tuple-element.20.home), custom_call_target="tpu_custom_call" | custom-call | flops 2000000 | bytes 400000 | tf_op jit(solution)/shard_map/ar_terms/pallas_call | solution.py:262
  55.5 0.0 collective-permute-done.4
  55.5 0.6 %add.43 = f32[8,512]{1,0:T(8,128)} add(f32[8,512]{1,0:T(8,128)S(1)} %ar_terms.1, f32[8,512]{1,0:T(8,128)S(1)} %collective-permute-done.4) | non-fusion elementwise | flops 4096 | bytes 49152 | tf_op jit(solution)/shard_map/add | solution.py:301
  56.1 0.0 all-to-all-done.1
  56.1 0.1 fusion.3
  56.2 0.0 copy-done.2
  56.2 0.0 copy-done.3
  56.2 0.6 %divide_subtract_fusion = (f32[48,64]{1,0:T(8,128)}, f32[48,64]{1,0:T(8,128)}, f32[48,64]{1,0:T(8,128)}) fusion(f32[48,64]{1,0:T(8,128)S(1)} %copy.13, f32[24,64]{1,0:T(8,128)S(1)} %get-tuple-element.22, f32[24,64]{1,0:T(8,128)S(1)} %get-tuple-element.21, f32[48,64]{1,0:T(8,128)S(1)} %copy-done.2, f32[48,64]{1,0:T(8,128)S(1)} %copy-done.3), kind=kLoop, calls=%fused_computation.6 | loop fusion | flops 46080 | bytes 86016 | tf_op jit(solution)/shard_map/sub | solution.py:310
  (6 shorter events, 0.1 us)
Async XLA Ops:
  5.9 48.6 %copy-start = (f32[10,64]{1,0:T(8,128)S(1)}, f32[10,64]{1,0:T(8,128)}, u32[]{:S(2)}) copy-start(f32[10,64]{1,0:T(8,128)} %weights.1) | copy-start | bytes 7684
  6.0 48.6 %copy-start.1 = (s32[10]{0:T(128)S(1)}, s32[10]{0:T(128)}, u32[]{:S(2)}) copy-start(s32[10]{0:T(128)} %lags.1) | copy-start | bytes 124
  6.0 50.2 %copy-start.2 = (f32[48,64]{1,0:T(8,128)S(1)}, f32[48,64]{1,0:T(8,128)}, u32[]{:S(2)}) copy-start(f32[48,64]{1,0:T(8,128)} %param.14) | copy-start | bytes 36868
  6.0 50.2 %copy-start.3 = (f32[48,64]{1,0:T(8,128)S(1)}, f32[48,64]{1,0:T(8,128)}, u32[]{:S(2)}) copy-start(f32[48,64]{1,0:T(8,128)} %param.15) | copy-start | bytes 36868
  6.0 3.8 %collective-permute-start = (f32[800,128]{1,0:T(8,128)S(1)}, f32[800,128]{1,0:T(8,128)S(1)}, u32[]{:S(2)}, u32[]{:S(2)}) collective-permute-start(f32[800,128]{1,0:T(8,128)S(1)} %get-tuple-element.11), channel_id=1, source_target_pairs={{0,1},{1,0},{2,3},{3,2},{4,5},{5,4},{6,7},{7,6},{8,9},{9,8},{10,11... | collective-permute-start | bytes 1228808 | tf_op jit(solution)/shard_map/ppermute | solution.py:285
  10.6 15.9 %all-to-all-start = ((f32[4,256,128]{2,1,0:T(8,128)}), f32[4,256,128]{2,1,0:T(8,128)S(1)}, u32[]{:S(2)}, u32[]{:S(2)}) async-start(f32[4,256,128]{2,1,0:T(8,128)} %pair_terms.1), calls=%async_computation | async-start | bytes 1048576 | tf_op jit(solution)/shard_map/all_to_all | solution.py:290
  15.4 6.1 %collective-permute-start.2 = (f32[2,2,8,512]{3,2,1,0:T(8,128)S(1)}, f32[2,2,8,512]{3,2,1,0:T(8,128)S(1)}, u32[]{:S(2)}, u32[]{:S(2)}) collective-permute-start(f32[2,2,8,512]{3,2,1,0:T(8,128)S(1)} %get-tuple-element.15), channel_id=1, source_target_pairs={{0,64},{64,0},{128,192},{192,128},{1,65},{65,1},{129,193},{193,129... | collective-permute-start | bytes 196616 | tf_op jit(solution)/shard_map/ppermute | solution.py:287
  21.6 17.3 %collective-permute-start.3 = (f32[2,8,512]{2,1,0:T(8,128)S(1)}, f32[2,8,512]{2,1,0:T(8,128)S(1)}, u32[]{:S(2)}, u32[]{:S(2)}) collective-permute-start(f32[2,8,512]{2,1,0:T(8,128)S(1)} %slice_bitcast_fusion), channel_id=1, source_target_pairs={{0,192},{192,0},{64,128},{128,64},{1,193},{193,1},{65,129},{129,65... | collective-permute-start | bytes 98312 | tf_op jit(solution)/shard_map/ppermute | solution.py:289
  27.2 28.9 %all-to-all-start.1 = ((f32[8,24,128]{2,1,0:T(8,128)}), f32[8,24,128]{2,1,0:T(8,128)S(1)}, u32[]{:S(2)}, u32[]{:S(2)}) async-start(f32[8,24,128]{2,1,0:T(8,128)} %get-tuple-element.12), calls=%async_computation.1 | async-start | bytes 196608 | tf_op jit(solution)/shard_map/all_to_all | solution.py:298
  38.9 16.6 %collective-permute-start.4 = (f32[8,512]{1,0:T(8,128)S(1)}, f32[8,512]{1,0:T(8,128)S(1)}, u32[]{:S(2)}, u32[]{:S(2)}) collective-permute-start(f32[8,512]{1,0:T(8,128)S(1)} %get-tuple-element.19), channel_id=1, source_target_pairs={{0,256},{256,0},{1,257},{257,1},{2,258},{258,2},{3,259},{259,3},{4... | collective-permute-start | bytes 49160 | tf_op jit(solution)/shard_map/ppermute | solution.py:291
  47.2 7.4 %collective-permute-start.1 = (f32[3,32,128]{2,1,0:T(8,128)S(1)}, f32[3,32,128]{2,1,0:T(8,128)S(1)}, u32[]{:S(2)}, u32[]{:S(2)}) collective-permute-start(f32[3,32,128]{2,1,0:T(8,128)S(1)} %get-tuple-element.13), channel_id=1, source_target_pairs={{0,8},{1,9},{2,10},{3,11},{8,16},{9,17},{10,18},{11,19},{16,24},{1... | collective-permute-start | bytes 147464 | tf_op jit(solution)/shard_map/ppermute | solution.py:297
